TPU v7x, 1024 devices: a whole 8x8x8 slice. The times are simulated.
1024 devices in a mesh: space: 16 (over y_lo, z), batch: 64 (over x, y_hi, core).
Axes of the slice: x: 8, y: 8 (y_hi: 4, y_lo: 2; y = y_hi * 2 + y_lo), z: 8, core: 2. Of those that a mesh axis runs over, the one named last changes fastest.
Arguments:
- volume: bfloat16 [64, 4, 128, 32, 128], P('batch', None, 'space'), may hold values from -6 to 6
- kernel: bfloat16 [32, 108], replicated, may hold values from -0.625 to 0.625
- bias: float32 [32], replicated, may hold values from -3 to 3
- cotangent: bfloat16 [64, 32, 64, 1024], P('batch', 'space'), may hold values from -0.062148057 to 0.062148057
Outputs:
- pooled: bfloat16 [64, 32, 64, 1024], P('batch', 'space')
- kernel_grad: float32 [32, 108], replicated
- bias_grad: float32 [32], replicated
All inputs are finite; a program needn't handle non-finite values.
Results may differ from a plain program's by a relative error of at most 0.0065.
Values may be sent and summed in bfloat16 or wider, within the bound.
No kernel may reach another device: no remote copies, remote signals or barrier semaphores. Data moves between devices by JAX's collectives and lax.ppermute only.
A program may use at most 32 MiB of HBM per device.

v0:
```python
import jax
import jax.numpy as jnp
from jax import lax
from jax.sharding import PartitionSpec as P

TAP_OFFSETS = [
    (first, second, third) for first in range(3) for second in range(3) for third in range(3)
]


def extended(block, sides, width):
    for axis, dim in sides:
        count = lax.axis_size(axis)
        forward = [(i, i + 1) for i in range(count - 1)]
        backward = [(target, source) for source, target in forward]
        low = lax.ppermute(
            lax.slice_in_dim(block, block.shape[dim] - width, None, axis=dim), axis, forward
        )
        high = lax.ppermute(lax.slice_in_dim(block, 0, width, axis=dim), axis, backward)
        block = jnp.concatenate([low, block, high], axis=dim)
    return block


def on_device(volume, kernel, bias, cotangent):
    local_volume = volume[0]
    channels_in, slab_depth, height, breadth = local_volume.shape
    outer = extended(local_volume, (("space", 1),), 1)
    padded = jnp.pad(outer, ((0, 0), (0, 0), (1, 1), (1, 1)))
    filters = kernel.shape[0]
    plane_cells = height * breadth // 4
    cells = 2 * height * breadth
    block_count = slab_depth // 2

    def compute_block(index, incoming):
        window = lax.dynamic_slice_in_dim(padded, index * 2, 4, 1)
        patches = jnp.concatenate(
            [
                window[:, sd : sd + 2, sh : sh + height, sw : sw + breadth]
                for sd, sh, sw in TAP_OFFSETS
            ],
            axis=0,
        ).reshape(27 * channels_in, cells)
        conv_out = jnp.dot(kernel, patches, preferred_element_type=jnp.float32) + bias[:, None]
        positive = conv_out > 0
        activated = jnp.where(positive, conv_out, 0.3 * conv_out).astype(jnp.bfloat16)
        pooled_block = activated.astype(jnp.float32).reshape(
            filters, 1, 2, height // 2, 2, breadth // 2, 2
        )
        pooled_block = (
            pooled_block.mean(axis=(2, 4, 6)).astype(jnp.bfloat16).reshape(filters, 1, plane_cells)
        )
        scaled = (
            incoming.astype(jnp.float32).reshape(filters, 1, 1, height // 2, 1, breadth // 2, 1)
            * 0.125
        )
        widened = jnp.broadcast_to(
            scaled, (filters, 1, 2, height // 2, 2, breadth // 2, 2)
        ).reshape(filters, cells)
        spread = (widened * jnp.where(positive, 1.0, 0.3)).astype(jnp.bfloat16)
        kernel_part = lax.dot_general(
            spread, patches, (((1,), (1,)), ((), ())), preferred_element_type=jnp.float32
        )
        bias_part = jnp.sum(spread.astype(jnp.float32), axis=1)
        return (pooled_block, kernel_part, bias_part)

    zero_kernel = jnp.zeros((filters, 27 * channels_in), jnp.float32)
    zero_bias = jnp.zeros((filters,), jnp.float32)
    returned = lax.all_to_all(cotangent[0], "space", split_axis=1, concat_axis=0, tiled=True)

    def advance(index, carry):
        pooled_buffer, kernel_sum, bias_sum = carry
        incoming = lax.dynamic_slice_in_dim(returned, index, 1, 1)
        pooled_block, kernel_part, bias_part = compute_block(index, incoming)
        pooled_buffer = lax.dynamic_update_slice_in_dim(pooled_buffer, pooled_block, index, 1)
        return (pooled_buffer, kernel_sum + kernel_part, bias_sum + bias_part)

    start_state = (
        jnp.zeros((filters, block_count, plane_cells), jnp.bfloat16),
        zero_kernel,
        zero_bias,
    )
    pooled_slab, kernel_sum, bias_sum = lax.fori_loop(0, block_count, advance, start_state)
    pooled_owned = lax.all_to_all(pooled_slab, "space", split_axis=0, concat_axis=1, tiled=True)
    kernel_grad, bias_grad = lax.psum((kernel_sum, bias_sum), ("space", "batch"))
    return (pooled_owned[None], kernel_grad, bias_grad)


def solution(mesh):
    placed = (P("batch", None, "space", None, None), P(), P(), P("batch", "space", None, None))
    return jax.shard_map(
        on_device,
        mesh=mesh,
        in_specs=placed,
        out_specs=(P("batch", "space", None, None), P(), P()),
        check_vma=False,
    )
```

profile of v0, /device:TPU:1, one launch (start us, length us, event | category | flops | bytes accessed | tf_op | source)
XLA Modules:
  0.0 260.2 jit_solution(5911412824895711319)
XLA Ops:
  0.7 1.9 copy.37
  2.6 18.5 %all-to-all-start = ((bf16[2,64,1024]{2,0,1:T(2,128)(2,1)}), bf16[2,64,1024]{2,0,1:T(2,128)(2,1)S(1)}, u32[]{:S(2)}, u32[]{:S(2)}) async-start(bf16[2,64,1024]{2,0,1:T(2,128)(2,1)} %bitcast.23), calls=%async_computation | async-start | bytes 524288 | tf_op jit(solution)/shard_map/all_to_all | solution.py:68
  21.0 0.8 fusion.13
  21.8 3.3 %collective-permute-start = (bf16[4,1,32,128]{3,2,1,0:T(8,128)(2,1)S(1)}, bf16[4,1,32,128]{3,2,1,0:T(8,128)(2,1)S(1)}, u32[]{:S(2)}, u32[]{:S(2)}) collective-permute-start(bf16[4,1,32,128]{3,2,1,0:T(8,128)(2,1)S(1)} %get-tuple-element.219), channel_id=1, source_target_pairs={{0,64},{64,128},{128,192},{192,256},{256,320},{320,384},{384,448},... | collective-permute-start | bytes 98312 | tf_op jit(solution)/shard_map/ppermute | solution.py:16
  25.1 1.3 collective-permute-start.1
  26.5 3.7 %collective-permute-done.1 = bf16[4,1,32,128]{3,2,1,0:T(8,128)(2,1)S(1)} collective-permute-done((bf16[4,1,32,128]{3,2,1,0:T(8,128)(2,1)S(1)}, bf16[4,1,32,128]{3,2,1,0:T(8,128)(2,1)S(1)}, u32[]{:S(2)}, u32[]{:S(2)}) %collective-permute-start.1) | collective-permute-done | bytes 32800 | tf_op jit(solution)/shard_map/ppermute | solution.py:19
  30.2 1.5 select_maximum_fusion
  31.9 101.5 %while.18 = (s32[]{:T(128)}, bf16[32,4,1024]{2,0,1:T(8,128)(2,1)}, f32[32,108]{1,0:T(8,128)S(1)}, f32[32]{0:T(128)S(1)}, bf16[4,10,34,130]{3,2,1,0:T(8,128)(2,1)...) while((s32[]{:T(128)}, bf16[32,4,1024]{2,0,1:T(8,128)(2,1)}, ...), condition=%wide.region_3.4_spmd.clone, body=%wide.region_0.3_spmd.clone.sunk | while | flops 116497192 | bytes 25267560 | solution.py:82
  34.6 0.1 pad.16
  34.8 1.5 copy.45
  36.3 0.1 constant_dynamic-slice_fusion.2
  36.4 0.2 copy.43
  36.7 4.0 %broadcast_in_dim.48 = f32[32,2,16,2,64,2]{0,5,4,3,2,1:T(2,128)} broadcast(f32[32,16,64]{0,2,1:T(8,128)S(1)} %bitcast.49), dimensions={0,2,4} | broadcast | bytes 1179648 | tf_op jit(solution)/shard_map/while/body/eval_jaxpr/broadcast_in_dim | solution.py:56
  40.7 3.6 %copy.44 = f32[32,8192]{1,0:T(8,128)} copy(f32[32,8192]{0,1:T(8,128)} %bitcast.45) | data formatting | bytes 2097152 | tf_op jit(solution)/shard_map/while/body/eval_jaxpr/broadcast_in_dim | solution.py:56
  44.3 2.8 %convert_reduce_fusion.2 = (f32[32]{0:T(128)S(1)}, bf16[32,8192]{1,0:T(8,128)(2,1)S(1)}, f32[32,8192]{1,0:T(8,128)}) fusion(f32[32,8192]{1,0:T(8,128)} %copy.44, f32[32]{0:T(128)S(1)} %get-tuple-element.314, bf16[108,8192]{1,0:T(8,128)(2,1)S(1)} %bitcast.46, bf16[32,108]{1,0:T(8,128)(2,1)S(1)} %get-tuple-element.313), kind=kOutput, calls=%fused_computation.8.clone.1 | convolution fusion | flops 59506656 | bytes 4398080 | tf_op jit(solution)/shard_map/while/body/eval_jaxpr/dot_general | solution.py:43
  47.0 0.7 convolution_add_fusion.3
  47.8 3.6 %copy.46 = f32[32,8192]{0,1:T(8,128)} copy(f32[32,8192]{1,0:T(8,128)} %get-tuple-element.273) | data formatting | bytes 2097152 | tf_op jit(solution)/shard_map/while/body/eval_jaxpr/reshape | solution.py:46
  51.4 4.8 %reduce_sum.30 = f32[32,16,64]{0,2,1:T(8,128)S(1)} reduce(f32[32,2,16,2,64,2]{0,5,4,3,2,1:T(2,128)} %bitcast.44, f32[]{:T(128)} %constant.66.clone.8..sunk), dimensions={1,3,5}, to_apply=%region_1.1 | reduce | flops 229376 | bytes 1179652 | tf_op jit(solution)/shard_map/while/body/eval_jaxpr/reduce_sum | solution.py:50
  56.2 0.2 copy.47
  56.5 0.1 convert_element_type.75
  56.6 0.6 constant_dynamic-update-slice_fusion.2
  60.0 0.1 pad.16
  60.1 1.5 copy.45
  61.7 0.1 constant_dynamic-slice_fusion.2
  61.8 0.2 copy.43
  62.0 4.0 %broadcast_in_dim.48 = f32[32,2,16,2,64,2]{0,5,4,3,2,1:T(2,128)} broadcast(f32[32,16,64]{0,2,1:T(8,128)S(1)} %bitcast.49), dimensions={0,2,4} | broadcast | bytes 1179648 | tf_op jit(solution)/shard_map/while/body/eval_jaxpr/broadcast_in_dim | solution.py:56
  66.0 3.6 %copy.44 = f32[32,8192]{1,0:T(8,128)} copy(f32[32,8192]{0,1:T(8,128)} %bitcast.45) | data formatting | bytes 2097152 | tf_op jit(solution)/shard_map/while/body/eval_jaxpr/broadcast_in_dim | solution.py:56
  69.6 2.8 %convert_reduce_fusion.2 = (f32[32]{0:T(128)S(1)}, bf16[32,8192]{1,0:T(8,128)(2,1)S(1)}, f32[32,8192]{1,0:T(8,128)}) fusion(f32[32,8192]{1,0:T(8,128)} %copy.44, f32[32]{0:T(128)S(1)} %get-tuple-element.314, bf16[108,8192]{1,0:T(8,128)(2,1)S(1)} %bitcast.46, bf16[32,108]{1,0:T(8,128)(2,1)S(1)} %get-tuple-element.313), kind=kOutput, calls=%fused_computation.8.clone.1 | convolution fusion | flops 59506656 | bytes 4398080 | tf_op jit(solution)/shard_map/while/body/eval_jaxpr/dot_general | solution.py:43
  72.4 0.7 convolution_add_fusion.3
  73.1 3.6 %copy.46 = f32[32,8192]{0,1:T(8,128)} copy(f32[32,8192]{1,0:T(8,128)} %get-tuple-element.273) | data formatting | bytes 2097152 | tf_op jit(solution)/shard_map/while/body/eval_jaxpr/reshape | solution.py:46
  76.7 4.8 %reduce_sum.30 = f32[32,16,64]{0,2,1:T(8,128)S(1)} reduce(f32[32,2,16,2,64,2]{0,5,4,3,2,1:T(2,128)} %bitcast.44, f32[]{:T(128)} %constant.66.clone.8..sunk), dimensions={1,3,5}, to_apply=%region_1.1 | reduce | flops 229376 | bytes 1179652 | tf_op jit(solution)/shard_map/while/body/eval_jaxpr/reduce_sum | solution.py:50
  81.6 0.2 copy.47
  81.9 0.1 convert_element_type.75
  82.0 0.6 constant_dynamic-update-slice_fusion.2
  85.4 0.1 pad.16
  85.5 1.5 copy.45
  87.0 0.1 constant_dynamic-slice_fusion.2
  87.2 0.2 copy.43
  87.4 4.0 %broadcast_in_dim.48 = f32[32,2,16,2,64,2]{0,5,4,3,2,1:T(2,128)} broadcast(f32[32,16,64]{0,2,1:T(8,128)S(1)} %bitcast.49), dimensions={0,2,4} | broadcast | bytes 1179648 | tf_op jit(solution)/shard_map/while/body/eval_jaxpr/broadcast_in_dim | solution.py:56
  91.4 3.6 %copy.44 = f32[32,8192]{1,0:T(8,128)} copy(f32[32,8192]{0,1:T(8,128)} %bitcast.45) | data formatting | bytes 2097152 | tf_op jit(solution)/shard_map/while/body/eval_jaxpr/broadcast_in_dim | solution.py:56
  95.0 2.8 %convert_reduce_fusion.2 = (f32[32]{0:T(128)S(1)}, bf16[32,8192]{1,0:T(8,128)(2,1)S(1)}, f32[32,8192]{1,0:T(8,128)}) fusion(f32[32,8192]{1,0:T(8,128)} %copy.44, f32[32]{0:T(128)S(1)} %get-tuple-element.314, bf16[108,8192]{1,0:T(8,128)(2,1)S(1)} %bitcast.46, bf16[32,108]{1,0:T(8,128)(2,1)S(1)} %get-tuple-element.313), kind=kOutput, calls=%fused_computation.8.clone.1 | convolution fusion | flops 59506656 | bytes 4398080 | tf_op jit(solution)/shard_map/while/body/eval_jaxpr/dot_general | solution.py:43
  97.8 0.7 convolution_add_fusion.3
  98.5 3.6 %copy.46 = f32[32,8192]{0,1:T(8,128)} copy(f32[32,8192]{1,0:T(8,128)} %get-tuple-element.273) | data formatting | bytes 2097152 | tf_op jit(solution)/shard_map/while/body/eval_jaxpr/reshape | solution.py:46
  102.1 4.8 %reduce_sum.30 = f32[32,16,64]{0,2,1:T(8,128)S(1)} reduce(f32[32,2,16,2,64,2]{0,5,4,3,2,1:T(2,128)} %bitcast.44, f32[]{:T(128)} %constant.66.clone.8..sunk), dimensions={1,3,5}, to_apply=%region_1.1 | reduce | flops 229376 | bytes 1179652 | tf_op jit(solution)/shard_map/while/body/eval_jaxpr/reduce_sum | solution.py:50
  107.0 0.2 copy.47
  107.2 0.1 convert_element_type.75
  107.4 0.6 constant_dynamic-update-slice_fusion.2
  110.7 0.1 pad.16
  110.9 1.5 copy.45
  112.4 0.1 constant_dynamic-slice_fusion.2
  112.5 0.2 copy.43
  112.8 4.0 %broadcast_in_dim.48 = f32[32,2,16,2,64,2]{0,5,4,3,2,1:T(2,128)} broadcast(f32[32,16,64]{0,2,1:T(8,128)S(1)} %bitcast.49), dimensions={0,2,4} | broadcast | bytes 1179648 | tf_op jit(solution)/shard_map/while/body/eval_jaxpr/broadcast_in_dim | solution.py:56
  116.7 3.6 %copy.44 = f32[32,8192]{1,0:T(8,128)} copy(f32[32,8192]{0,1:T(8,128)} %bitcast.45) | data formatting | bytes 2097152 | tf_op jit(solution)/shard_map/while/body/eval_jaxpr/broadcast_in_dim | solution.py:56
  120.4 2.8 %convert_reduce_fusion.2 = (f32[32]{0:T(128)S(1)}, bf16[32,8192]{1,0:T(8,128)(2,1)S(1)}, f32[32,8192]{1,0:T(8,128)}) fusion(f32[32,8192]{1,0:T(8,128)} %copy.44, f32[32]{0:T(128)S(1)} %get-tuple-element.314, bf16[108,8192]{1,0:T(8,128)(2,1)S(1)} %bitcast.46, bf16[32,108]{1,0:T(8,128)(2,1)S(1)} %get-tuple-element.313), kind=kOutput, calls=%fused_computation.8.clone.1 | convolution fusion | flops 59506656 | bytes 4398080 | tf_op jit(solution)/shard_map/while/body/eval_jaxpr/dot_general | solution.py:43
  123.1 0.7 convolution_add_fusion.3
  123.9 3.6 %copy.46 = f32[32,8192]{0,1:T(8,128)} copy(f32[32,8192]{1,0:T(8,128)} %get-tuple-element.273) | data formatting | bytes 2097152 | tf_op jit(solution)/shard_map/while/body/eval_jaxpr/reshape | solution.py:46
  127.5 4.8 %reduce_sum.30 = f32[32,16,64]{0,2,1:T(8,128)S(1)} reduce(f32[32,2,16,2,64,2]{0,5,4,3,2,1:T(2,128)} %bitcast.44, f32[]{:T(128)} %constant.66.clone.8..sunk), dimensions={1,3,5}, to_apply=%region_1.1 | reduce | flops 229376 | bytes 1179652 | tf_op jit(solution)/shard_map/while/body/eval_jaxpr/reduce_sum | solution.py:50
  132.3 0.2 copy.47
  132.6 0.1 convert_element_type.75
  132.7 0.6 constant_dynamic-update-slice_fusion.2
  133.4 1.8 copy.32
  135.2 7.2 %all-to-all-start.1 = ((bf16[32,4,1024]{2,1,0:T(4,128)(2,1)}), bf16[32,4,1024]{2,1,0:T(4,128)(2,1)S(1)}, u32[]{:S(2)}, u32[]{:S(2)}) async-start(bf16[32,4,1024]{2,1,0:T(4,128)(2,1)} %copy.32), calls=%async_computation.1 | async-start | bytes 524288 | tf_op jit(solution)/shard_map/all_to_all | solution.py:83
  142.5 116.9 %all-reduce.1 = (f32[32,108]{1,0:T(8,128)}, f32[32]{0:T(128)}) all-reduce(f32[32,108]{1,0:T(8,128)S(1)} %get-tuple-element.145, f32[32]{0:T(128)S(1)} %get-tuple-element.146), channel_id=1, replica_groups=mesh['space'=16,'batch'=64] {'space','batch'}, use_global_device_ids=true, to_apply=%region_4.5 | all-reduce | flops 3488 | bytes 27904 | tf_op jit(solution)/shard_map/psum | solution.py:84
  259.5 0.8 broadcast_in_dim.41
  (132 shorter events, 11.2 us)
Async XLA Ops:
  0.6 31.2 %copy-start = (bf16[32,108]{1,0:T(8,128)(2,1)S(1)}, bf16[32,108]{1,0:T(8,128)(2,1)}, u32[]{:S(2)}) copy-start(bf16[32,108]{1,0:T(8,128)(2,1)} %param.7) | copy-start | bytes 20740
  0.6 31.2 %copy-start.1 = (f32[32]{0:T(128)S(1)}, f32[32]{0:T(128)}, u32[]{:S(2)}) copy-start(f32[32]{0:T(128)} %param.8) | copy-start | bytes 388
  2.6 29.2 %all-to-all-start = ((bf16[2,64,1024]{2,0,1:T(2,128)(2,1)}), bf16[2,64,1024]{2,0,1:T(2,128)(2,1)S(1)}, u32[]{:S(2)}, u32[]{:S(2)}) async-start(bf16[2,64,1024]{2,0,1:T(2,128)(2,1)} %bitcast.23), calls=%async_computation | async-start | bytes 524288 | tf_op jit(solution)/shard_map/all_to_all | solution.py:68
  21.8 4.7 %collective-permute-start = (bf16[4,1,32,128]{3,2,1,0:T(8,128)(2,1)S(1)}, bf16[4,1,32,128]{3,2,1,0:T(8,128)(2,1)S(1)}, u32[]{:S(2)}, u32[]{:S(2)}) collective-permute-start(bf16[4,1,32,128]{3,2,1,0:T(8,128)(2,1)S(1)} %get-tuple-element.219), channel_id=1, source_target_pairs={{0,64},{64,128},{128,192},{192,256},{256,320},{320,384},{384,448},... | collective-permute-start | bytes 98312 | tf_op jit(solution)/shard_map/ppermute | solution.py:16
  25.1 5.1 %collective-permute-start.1 = (bf16[4,1,32,128]{3,2,1,0:T(8,128)(2,1)S(1)}, bf16[4,1,32,128]{3,2,1,0:T(8,128)(2,1)S(1)}, u32[]{:S(2)}, u32[]{:S(2)}) collective-permute-start(bf16[4,1,32,128]{3,2,1,0:T(8,128)(2,1)S(1)} %get-tuple-element.220), channel_id=1, source_target_pairs={{64,0},{128,64},{192,128},{256,192},{320,256},{384,320},{448,384},... | collective-permute-start | bytes 98312 | tf_op jit(solution)/shard_map/ppermute | solution.py:19
  135.2 124.1 %all-to-all-start.1 = ((bf16[32,4,1024]{2,1,0:T(4,128)(2,1)}), bf16[32,4,1024]{2,1,0:T(4,128)(2,1)S(1)}, u32[]{:S(2)}, u32[]{:S(2)}) async-start(bf16[32,4,1024]{2,1,0:T(4,128)(2,1)} %copy.32), calls=%async_computation.1 | async-start | bytes 524288 | tf_op jit(solution)/shard_map/all_to_all | solution.py:83
where the time goes:
time: 261 us; the launch traced here: 260 us
  blocking collectives  117 us (45%)
  local copies, waits for them, and re-layouts  72.7 us (28%)
  starting transfers between devices  30.2 us (12%)
  other arithmetic  21.2 us (8%)
  matrix products  14 us (5%)
  waiting for transfers between devices  3.78 us (1%)
    psum x1, blocking collectives, on_device(): lax.psum((kernel_sum, bias_sum), ('space', 'batch'))  117 us
    broadcast_in_dim x8, local copies, waits for them, and re-layouts, compute_block(): jnp.broadcast_to(scaled, (filters, 1, 2, height // 2, 2, breadth // 2, 2))  30.3 us
    reduce_sum x4, other arithmetic, compute_block(): pooled_block.mean(axis=(2, 4, 6)).astype(jnp.bfloat16)  19.4 us
    all_to_all x1, starting transfers between devices, on_device(): lax.all_to_all(cotangent[0], 'space', split_axis=1, concat_axis=0, tiled=...  18.5 us
    while x112, local copies, waits for them, and re-layouts  16.6 us
    reshape x4, local copies, waits for them, and re-layouts, compute_block(): activated.astype(jnp.float32)  14.4 us
    dot_general x4, matrix products, compute_block(): jnp.dot(kernel, patches, preferred_element_type=jnp.float32) + bias[:, None]  11.1 us
    all_to_all x1, starting transfers between devices, on_device(): lax.all_to_all(pooled_slab, 'space', split_axis=0, concat_axis=1, tiled=T...  7.24 us
  transfers between devices with their start and end apart: 4, of which 2 were waited for; matrix products, arithmetic and copies ran while one was open for 1% of the time, Pallas kernels for 0%

commit v1 on v0

v1 whole, which is shorter than its diff:
```python
import jax
import jax.numpy as jnp
import numpy as np
from jax import lax
from jax.experimental import pallas as pl
from jax.experimental.pallas import tpu as pltpu
from jax.sharding import PartitionSpec as P

CLASSES = [(pd, ph, pw) for pd in range(2) for ph in range(2) for pw in range(2)]
CHANNELS = 4
FILTERS = 32
TAPS = 27 * CHANNELS
ROWS = 48


def window_shift(pd, ph, pw):
    return ph * 64 + pw * 16 + pd * 4


def tap_table():
    table = np.zeros((128, 256), np.float32)
    for a in range(3):
        for b in range(3):
            for e in range(3):
                for c in range(CHANNELS):
                    table[(a * 9 + b * 3 + e) * CHANNELS + c, b * 64 + e * 16 + a * 4 + c] = 1.0
    return table


def width_table():
    table = np.zeros((2, 128, 4, 2, 64), np.float32)
    for half in range(2):
        for k in range(4):
            for cell in range(64):
                w = 2 * cell - 1 + k
                if 0 <= w < 128:
                    table[half, w, k, half, cell] = 1.0
    return table.reshape(256, 512)


def row_table(order):
    table = np.zeros((128, 128), np.float32)
    table[np.arange(128), order] = 1.0
    return table


def slab_kernel(
    vol_ref, low_ref, high_ref, kern_ref, bias_ref, cot_ref, taps_ref, width_ref, order_ref, back_ref,
    out_ref, flat, lines, split, window, spread, pooled, cots
):
    f32, bf16 = jnp.float32, jnp.bfloat16
    for c in range(CHANNELS):
        for d in range(10):
            if d == 0:
                plane = low_ref[c, 0]
            elif d == 9:
                plane = high_ref[c, 0]
            else:
                plane = vol_ref[c, d - 1]
            flat[(d * CHANNELS + c) * 32 : (d * CHANNELS + c + 1) * 32, :] = plane.astype(f32)
    zero_line = jnp.zeros((ROWS, 128), bf16)
    lines[0, :, 0:128] = zero_line
    lines[31, :, 128:256] = zero_line
    for h in range(32):
        line = flat[pl.ds(h, 40, stride=32), :]
        line = jnp.concatenate([line, jnp.zeros((8, 128), f32)], axis=0).astype(bf16)
        if h <= 30:
            h4, j = divmod(h + 1, 4)
            lines[j * 8 + h4, :, 0:128] = line
        if h >= 1:
            h4, j = divmod(h - 1, 4)
            lines[j * 8 + h4, :, 128:256] = line
    for j in range(4):
        rows = lines[j * 8 : (j + 1) * 8].reshape(8 * ROWS, 256)
        split[j] = jnp.dot(rows, width_ref[...], preferred_element_type=f32)
    for d2 in range(4):
        for h4 in range(8):
            for j in range(4):
                for k in range(4):
                    first = h4 * ROWS + d2 * 8
                    window[
                        (j * 4 + k) * 16 : (j * 4 + k + 1) * 16,
                        (d2 * 8 + h4) * 128 : (d2 * 8 + h4 + 1) * 128,
                    ] = split[j, first : first + 16, k * 128 : (k + 1) * 128].astype(bf16)

    spread_taps = jnp.dot(kern_ref[...], taps_ref[...], preferred_element_type=f32)
    weights = jnp.concatenate(
        [
            pltpu.roll(spread_taps, window_shift(*parity), 1) if window_shift(*parity) else spread_taps
            for parity in CLASSES
        ],
        axis=0,
    ).astype(bf16)

    cots[...] = jnp.dot(order_ref[...], cot_ref[...], preferred_element_type=f32)
    bias = jnp.broadcast_to(bias_ref[...], (FILTERS, 128))
    bias_sum = jnp.zeros((FILTERS, 128), f32)
    for d2 in range(4):
        for tile in range(4):
            first = d2 * 1024 + tile * 256
            conv = jnp.dot(weights, window[:, first : first + 256], preferred_element_type=f32)
            for half in range(2):
                lane = tile * 256 + half * 128
                incoming = cots[d2 * FILTERS : (d2 + 1) * FILTERS, lane : lane + 128] * 0.125
                full = incoming.astype(bf16).astype(f32)
                part = (incoming * 0.3).astype(bf16).astype(f32)
                total = jnp.zeros((FILTERS, 128), f32)
                for n in range(8):
                    x = conv[n * FILTERS : (n + 1) * FILTERS, half * 128 : (half + 1) * 128] + bias
                    total = total + jnp.maximum(x, 0.3 * x).astype(bf16).astype(f32)
                    back = jnp.where(x > 0, full, part)
                    bias_sum = bias_sum + back
                    spread[
                        n * FILTERS : (n + 1) * FILTERS,
                        first + half * 128 : first + (half + 1) * 128,
                    ] = back.astype(bf16)
                pooled[d2 * FILTERS : (d2 + 1) * FILTERS, lane : lane + 128] = (total * 0.125).astype(bf16)

    out_ref[:, 0:1024] = jnp.dot(back_ref[...], pooled[...], preferred_element_type=f32).astype(bf16)

    grads = lax.dot_general(
        spread[...], window[...], (((1,), (1,)), ((), ())), preferred_element_type=f32
    )
    folded = jnp.zeros((FILTERS, 256), f32)
    for n, parity in enumerate(CLASSES):
        shift = window_shift(*parity)
        block = grads[n * FILTERS : (n + 1) * FILTERS]
        folded = folded + (pltpu.roll(block, 256 - shift, 1) if shift else block)

    def pieces(value):
        one = value.astype(bf16)
        rest = value - one.astype(f32)
        two = rest.astype(bf16)
        three = (rest - two.astype(f32)).astype(bf16)
        return one, two, three

    bias_column = jnp.sum(bias_sum, axis=1, keepdims=True)
    columns = lax.broadcasted_iota(jnp.int32, (FILTERS, 128), 1)
    sent = []
    for taps, own in zip(pieces(folded), pieces(bias_column), strict=True):
        picked = lax.dot_general(taps, taps_ref[...], (((1,), (1,)), ((), ())), preferred_element_type=f32)
        sent.append(jnp.where(columns == TAPS, own.astype(f32), picked))
    sent.append(jnp.zeros((FILTERS, 128), f32))
    stacked = jnp.concatenate(sent, axis=0).astype(bf16)
    out_ref[:, 1024:1152] = jnp.dot(back_ref[...], stacked, preferred_element_type=f32).astype(bf16)


def slab(volume, low, high, kernel, bias, cots):
    f32, bf16 = jnp.float32, jnp.bfloat16
    by_depth = np.array([o * 4 + d for d in range(4) for o in range(FILTERS)])
    by_filter = np.argsort(by_depth)
    taps = jnp.asarray(tap_table(), bf16)
    width = jnp.asarray(width_table(), bf16)
    order = jnp.asarray(row_table(by_depth), bf16)
    back = jnp.asarray(row_table(by_filter), bf16)
    padded = jnp.pad(kernel, ((0, 0), (0, 128 - TAPS)))
    operands = (volume, low, high, padded, bias[:, None], cots, taps, width, order, back)
    return pl.pallas_call(
        slab_kernel,
        out_shape=jax.ShapeDtypeStruct((128, 1152), bf16),
        in_specs=[pl.BlockSpec(memory_space=pltpu.VMEM)] * len(operands),
        out_specs=pl.BlockSpec(memory_space=pltpu.VMEM),
        scratch_shapes=[
            pltpu.VMEM((1280, 128), f32),
            pltpu.VMEM((32, ROWS, 256), bf16),
            pltpu.VMEM((4, 8 * ROWS, 512), f32),
            pltpu.VMEM((256, 4096), bf16),
            pltpu.VMEM((256, 4096), bf16),
            pltpu.VMEM((128, 1024), bf16),
            pltpu.VMEM((128, 1024), f32),
        ],
        compiler_params=pltpu.CompilerParams(vmem_limit_bytes=24 * 1024 * 1024),
        cost_estimate=pl.CostEstimate(flops=1_500_000_000, bytes_accessed=2_000_000, transcendentals=0),
    )(*operands)


def reorder(order, rows):
    return jnp.dot(jnp.asarray(row_table(order), rows.dtype), rows, preferred_element_type=rows.dtype)


def on_device(volume, kernel, bias, cotangent):
    f32 = jnp.float32
    spaces, batches = lax.axis_size("space"), lax.axis_size("batch")
    owned_rows = np.arange(128).reshape(2, spaces, 4)
    to_slabs = owned_rows.transpose(1, 0, 2).reshape(-1)
    to_owner = np.argsort(to_slabs)

    up = [(i, i + 1) for i in range(spaces - 1)]
    down = [(i + 1, i) for i in range(spaces - 1)]
    local = volume[0]
    sent = reorder(to_slabs, cotangent.reshape(128, 1024))
    low = lax.ppermute(local[:, -1:], "space", up)
    high = lax.ppermute(local[:, :1], "space", down)
    cots = lax.all_to_all(sent, "space", split_axis=0, concat_axis=0, tiled=True)

    out = slab(local, low, high, kernel, bias, cots)

    out = lax.all_to_all(out, "space", split_axis=0, concat_axis=0, tiled=True)
    pooled = reorder(to_owner, out[:, :1024]).reshape(1, 2, 64, 1024)
    terms = jnp.sum(out[:, 1024:].reshape(spaces, 2, 4, 128).astype(f32), axis=(0, 2))
    terms = lax.all_to_all(
        jnp.broadcast_to(terms[None], (batches, 2, 128)), "batch", split_axis=0, concat_axis=0, tiled=True
    )
    terms = jnp.sum(terms, axis=0)
    terms = lax.all_to_all(
        jnp.broadcast_to(terms[None], (spaces, 2, 128)), "space", split_axis=0, concat_axis=0, tiled=True
    ).reshape(FILTERS, 128)
    return (pooled, terms[:, :TAPS], terms[:, TAPS])


def solution(mesh):
    placed = (P("batch", None, "space", None, None), P(), P(), P("batch", "space", None, None))
    return jax.shard_map(
        on_device,
        mesh=mesh,
        in_specs=placed,
        out_specs=(P("batch", "space", None, None), P(), P()),
        check_vma=False,
    )
```

time: 261 us -> 92.7 us (0.36)
  blocking collectives: 117 us -> 43.6 us
  local copies, waits for them, and re-layouts: 72.7 us -> 3.03 us
  other arithmetic: 21.2 us -> 0.11 us
  matrix products: 14 us -> 2.6 us
  waiting for transfers between devices: 3.78 us -> 9.24 us
  Pallas kernels: 0 us -> 4.61 us
    psum x1 -> x0, blocking collectives: 117 us -> none  [on_device(): lax.psum((kernel_sum, bias_sum), ('space', 'batch'))]
    all_to_all x0 -> x2, blocking collectives: none -> 43.6 us  [the longest x1 28.6 us: on_device(): lax.all_to_all(jnp.broadcast_to(terms[None], (batches, 2, 128)), 'batch',...]
    broadcast_in_dim x9 -> x3, local copies, waits for them, and re-layouts: 31.1 us -> 0.72 us  [the longest x1 0.61 us: on_device(): jnp.broadcast_to(terms[None], (spaces, 2, 128))]
    reduce_sum x4 -> x2, other arithmetic: 19.4 us -> 0.11 us  [the longest x1 0.08 us: on_device(): terms = jnp.sum(terms, axis=0)]
    while x113 -> x0, local copies, waits for them, and re-layouts: 18.5 us -> none
    reshape x4 -> x0, local copies, waits for them, and re-layouts: 14.4 us -> none  [compute_block(): activated.astype(jnp.float32)]
    dot_general x8 -> x2, matrix products: 14 us -> 2.6 us  [reorder(): jnp.dot(jnp.asarray(row_table(order), rows.dtype), rows, preferred_elemen...]
    all_to_all x2, waiting for transfers between devices: 0.01 us -> 6.41 us  [the longest x1 6.41 us: on_device(): lax.all_to_all(jnp.broadcast_to(terms[None], (spaces, 2, 128)), 'space',...]
where the time goes in v1:
time: 92.7 us; the launch traced here: 92.2 us
  blocking collectives  43.6 us (47%)
  starting transfers between devices  28.3 us (31%)
  waiting for transfers between devices  9.24 us (10%)
  Pallas kernels  4.61 us (5%)
  local copies, waits for them, and re-layouts  3.03 us (3%)
  matrix products  2.6 us (3%)
    all_to_all x1, blocking collectives, on_device(): lax.all_to_all(jnp.broadcast_to(terms[None], (batches, 2, 128)), 'batch',...  28.6 us
    all_to_all x1, starting transfers between devices, on_device(): lax.all_to_all(sent, 'space', split_axis=0, concat_axis=0, tiled=True)  18.6 us
    all_to_all x1, blocking collectives, on_device(): out = lax.all_to_all(out, 'space', split_axis=0, concat_axis=0, tiled=True)  15 us
    all_to_all x1, waiting for transfers between devices, on_device(): lax.all_to_all(jnp.broadcast_to(terms[None], (spaces, 2, 128)), 'space',...  6.41 us
    pallas_call x1, Pallas kernels, slab(): pl.pallas_call(slab_kernel, out_shape=jax.ShapeDtypeStruct((128, 1152), b...  4.61 us
    all_to_all x1, starting transfers between devices, on_device(): lax.all_to_all(jnp.broadcast_to(terms[None], (spaces, 2, 128)), 'space',...  4.29 us
    ppermute x1, starting transfers between devices, on_device(): low = lax.ppermute(local[:, -1:], 'space', up)  3.99 us
    ppermute x1, waiting for transfers between devices, on_device(): high = lax.ppermute(local[:, :1], 'space', down)  2.83 us
  transfers between devices with their start and end apart: 4, of which 2 were waited for; matrix products, arithmetic and copies ran while one was open for 1% of the time, Pallas kernels for 0%

profile of v1, /device:TPU:1, one launch (start us, length us, event | category | flops | bytes accessed | tf_op | source)
XLA Modules:
  0.0 92.2 jit_solution(4499717122977915215)
XLA Ops:
  0.6 0.0 copy-start
  0.6 0.9 %copy-done = bf16[1,2,64,1024]{3,2,1,0:T(8,128)(2,1)S(1)} copy-done((bf16[1,2,64,1024]{3,2,1,0:T(8,128)(2,1)S(1)}, bf16[1,2,64,1024]{3,2,1,0:T(8,128)(2,1)}, u32[]{:S(2)}) %copy-start) | copy-done | bytes 262168
  1.6 1.7 %fusion.3 = bf16[16,8,1024]{2,1,0:T(8,128)(2,1)} fusion(bf16[16,8,128]{2,1,0:T(8,128)(2,1)} %constant.27, bf16[128,1024,1]{1,0,2:T(8,128)(2,1)S(1)} %bitcast.16), kind=kOutput, calls=%fused_computation.5 | convolution fusion | flops 33554432 | bytes 557056 | tf_op jit(solution)/shard_map/dot_general | solution.py:178
  3.3 0.0 copy-start.1
  3.3 0.0 copy-start.2
  3.3 18.6 %all-to-all-start = ((bf16[16,8,1024]{2,1,0:T(8,128)(2,1)}), bf16[16,8,1024]{2,1,0:T(8,128)(2,1)S(1)}, u32[]{:S(2)}, u32[]{:S(2)}) async-start(bf16[16,8,1024]{2,1,0:T(8,128)(2,1)} %fusion.3), calls=%async_computation | async-start | bytes 524288 | tf_op jit(solution)/shard_map/all_to_all | solution.py:194
  21.9 0.0 copy-done.1
  21.9 0.0 copy-start.8
  21.9 0.0 copy-start.7
  21.9 0.0 copy-start.3
  21.9 0.0 copy-start.5
  21.9 0.0 copy-start.4
  21.9 1.4 %collective-permute-start.1 = (bf16[4,1,32,128]{3,2,1,0:T(8,128)(2,1)S(1)}, bf16[4,1,32,128]{3,2,1,0:T(8,128)(2,1)S(1)}, u32[]{:S(2)}, u32[]{:S(2)}) collective-permute-start(bf16[4,1,32,128]{3,2,1,0:T(8,128)(2,1)S(1)} %get-tuple-element.3), channel_id=1, source_target_pairs={{64,0},{128,64},{192,128},{256,192},{320,256},{384,320},{448,384},... | collective-permute-start | bytes 98312 | tf_op jit(solution)/shard_map/ppermute | solution.py:193
  23.4 4.0 %collective-permute-start = (bf16[4,1,32,128]{3,2,1,0:T(8,128)(2,1)S(1)}, bf16[4,1,32,128]{3,2,1,0:T(8,128)(2,1)S(1)}, u32[]{:S(2)}, u32[]{:S(2)}) collective-permute-start(bf16[4,1,32,128]{3,2,1,0:T(8,128)(2,1)S(1)} %get-tuple-element.4), channel_id=1, source_target_pairs={{0,64},{64,128},{128,192},{192,256},{256,320},{320,384},{384,448},... | collective-permute-start | bytes 98312 | tf_op jit(solution)/shard_map/ppermute | solution.py:192
  27.4 0.0 copy-done.8
  27.4 0.1 copy.16.bias_ref
  27.5 0.0 copy-done.7
  27.5 2.8 %collective-permute-done.1.high_ref = bf16[4,1,32,128]{3,2,1,0:T(8,128)(2,1)S(1)} collective-permute-done((bf16[4,1,32,128]{3,2,1,0:T(8,128)(2,1)S(1)}, bf16[4,1,32,128]{3,2,1,0:T(8,128)(2,1)S(1)}, u32[]{:S(2)}, u32[]{:S(2)}) %collective-permute-start.1) | collective-permute-done | bytes 32800 | tf_op jit(solution)/shard_map/ppermute | solution.py:193
  30.3 0.0 collective-permute-done.low_ref
  30.3 0.0 all-to-all-done
  30.3 0.0 copy-done.2
  30.3 0.0 copy-done.3
  30.3 0.0 copy-done.5
  30.3 0.0 copy-done.4
  30.4 4.6 %shard_map.121 = bf16[128,1152]{1,0:T(8,128)(2,1)S(1)} custom-call(bf16[4,8,32,128]{3,2,1,0:T(8,128)(2,1)S(1)} %bitcast.20, bf16[4,1,32,128]{3,2,1,0:T(8,128)(2,1)S(1)} %collective-permute-done.low_ref, bf16[4,1,32,128]{3,2,1,0:T(8,128)(2,1)S(1)} %collective-permute-done.1.high_ref, bf16[32,128]{1,0:T(8,128)(2,1)S(1)} %pad.4.kern_ref, ...), custom_call_target="tpu_custom_call" | custom-call | flops 1500000000 | bytes 2000000 | tf_op jit(solution)/shard_map/pallas_call | solution.py:158
  35.0 15.0 %all_to_all.30 = bf16[16,8,1152]{2,1,0:T(8,128)(2,1)S(1)} all-to-all(bf16[16,8,1152]{2,1,0:T(8,128)(2,1)S(1)} %bitcast.17), channel_id=1, replica_groups=mesh['space'=16,'batch'=64] {'space'}, dimensions={0} | all-to-all | bytes 589824 | tf_op jit(solution)/shard_map/all_to_all | solution.py:198
  50.0 28.6 %all_to_all.31 = f32[64,2,128]{2,1,0:T(2,128)S(1)} all-to-all(f32[64,2,128]{2,1,0:T(2,128)S(1)} %broadcast_in_dim.7), channel_id=1, replica_groups=mesh['space'=16,'batch'=64] {'batch'}, dimensions={0} | all-to-all | bytes 131072 | tf_op jit(solution)/shard_map/all_to_all | solution.py:201
  78.6 0.1 reduce_sum.19
  78.7 0.0 copy-start.6
  78.7 0.6 broadcast_in_dim.8
  79.3 4.3 %all-to-all-start.3 = ((f32[16,2,128]{2,1,0:T(2,128)}), f32[16,2,128]{2,1,0:T(2,128)S(1)}, u32[]{:S(2)}, u32[]{:S(2)}) async-start(f32[16,2,128]{2,1,0:T(2,128)} %broadcast_in_dim.8), calls=%async_computation.3 | async-start | bytes 32768 | tf_op jit(solution)/shard_map/all_to_all | solution.py:205
  83.6 0.0 copy-done.6
  83.6 0.9 fusion
  84.5 6.4 %all-to-all-done.3 = f32[16,2,128]{2,1,0:T(2,128)S(1)} async-done(((f32[16,2,128]{2,1,0:T(2,128)}), f32[16,2,128]{2,1,0:T(2,128)S(1)}, u32[]{:S(2)}, u32[]{:S(2)}) %all-to-all-start.3) | async-done | bytes 16416 | tf_op jit(solution)/shard_map/all_to_all | solution.py:205
  90.9 0.7 slice_reduce_fusion
  91.6 0.6 copy.20
  (5 shorter events, 0.1 us)
Async XLA Ops:
  0.6 1.0 %copy-start = (bf16[1,2,64,1024]{3,2,1,0:T(8,128)(2,1)S(1)}, bf16[1,2,64,1024]{3,2,1,0:T(8,128)(2,1)}, u32[]{:S(2)}) copy-start(bf16[1,2,64,1024]{3,2,1,0:T(8,128)(2,1)} %param.13) | copy-start | bytes 786436
  3.3 18.6 %copy-start.1 = (bf16[1,4,8,32,128]{4,3,2,1,0:T(8,128)(2,1)S(1)}, bf16[1,4,8,32,128]{4,3,2,1,0:T(8,128)(2,1)}, u32[]{:S(2)}) copy-start(bf16[1,4,8,32,128]{4,3,2,1,0:T(8,128)(2,1)} %param.10) | copy-start | bytes 786436
  3.3 27.0 %copy-start.2 = (bf16[256,512]{1,0:T(8,128)(2,1)S(1)}, bf16[256,512]{1,0:T(8,128)(2,1)}, u32[]{:S(2)}) copy-start(bf16[256,512]{1,0:T(8,128)(2,1)} %constant.19.clone.width_ref) | copy-start | bytes 786436
  3.3 27.0 %all-to-all-start = ((bf16[16,8,1024]{2,1,0:T(8,128)(2,1)}), bf16[16,8,1024]{2,1,0:T(8,128)(2,1)S(1)}, u32[]{:S(2)}, u32[]{:S(2)}) async-start(bf16[16,8,1024]{2,1,0:T(8,128)(2,1)} %fusion.3), calls=%async_computation | async-start | bytes 524288 | tf_op jit(solution)/shard_map/all_to_all | solution.py:194
  21.9 5.5 %copy-start.8 = (f32[32]{0:T(128)S(1)}, f32[32]{0:T(128)}, u32[]{:S(2)}) copy-start(f32[32]{0:T(128)} %param.12) | copy-start | bytes 388
  21.9 5.6 %copy-start.7 = (bf16[32,108]{1,0:T(8,128)(2,1)S(1)}, bf16[32,108]{1,0:T(8,128)(2,1)}, u32[]{:S(2)}) copy-start(bf16[32,108]{1,0:T(8,128)(2,1)} %param.11) | copy-start | bytes 20740
  21.9 8.4 %copy-start.3 = (bf16[128,256]{1,0:T(8,128)(2,1)S(1)}, bf16[128,256]{1,0:T(8,128)(2,1)}, u32[]{:S(2)}) copy-start(bf16[128,256]{1,0:T(8,128)(2,1)} %constant.18.clone.taps_ref) | copy-start | bytes 196612
  21.9 8.4 %copy-start.5 = (bf16[128,128]{1,0:T(8,128)(2,1)S(1)}, bf16[128,128]{1,0:T(8,128)(2,1)}, u32[]{:S(2)}) copy-start(bf16[128,128]{1,0:T(8,128)(2,1)} %constant.20.clone.order_ref) | copy-start | bytes 98308
  21.9 8.4 %copy-start.4 = (bf16[128,128]{1,0:T(8,128)(2,1)S(1)}, bf16[128,128]{1,0:T(8,128)(2,1)}, u32[]{:S(2)}) copy-start(bf16[128,128]{1,0:T(8,128)(2,1)} %constant.21.clone.back_ref) | copy-start | bytes 98308
  21.9 8.4 %collective-permute-start.1 = (bf16[4,1,32,128]{3,2,1,0:T(8,128)(2,1)S(1)}, bf16[4,1,32,128]{3,2,1,0:T(8,128)(2,1)S(1)}, u32[]{:S(2)}, u32[]{:S(2)}) collective-permute-start(bf16[4,1,32,128]{3,2,1,0:T(8,128)(2,1)S(1)} %get-tuple-element.3), channel_id=1, source_target_pairs={{64,0},{128,64},{192,128},{256,192},{320,256},{384,320},{448,384},... | collective-permute-start | bytes 98312 | tf_op jit(solution)/shard_map/ppermute | solution.py:193
  23.4 6.9 %collective-permute-start = (bf16[4,1,32,128]{3,2,1,0:T(8,128)(2,1)S(1)}, bf16[4,1,32,128]{3,2,1,0:T(8,128)(2,1)S(1)}, u32[]{:S(2)}, u32[]{:S(2)}) collective-permute-start(bf16[4,1,32,128]{3,2,1,0:T(8,128)(2,1)S(1)} %get-tuple-element.4), channel_id=1, source_target_pairs={{0,64},{64,128},{128,192},{192,256},{256,320},{320,384},{384,448},... | collective-permute-start | bytes 98312 | tf_op jit(solution)/shard_map/ppermute | solution.py:192
  78.7 4.9 %copy-start.6 = (bf16[128,128]{1,0:T(8,128)(2,1)S(1)}, bf16[128,128]{1,0:T(8,128)(2,1)}, u32[]{:S(2)}) copy-start(bf16[128,128]{1,0:T(8,128)(2,1)} %constant.22.clone) | copy-start | bytes 98308
  79.3 11.6 %all-to-all-start.3 = ((f32[16,2,128]{2,1,0:T(2,128)}), f32[16,2,128]{2,1,0:T(2,128)S(1)}, u32[]{:S(2)}, u32[]{:S(2)}) async-start(f32[16,2,128]{2,1,0:T(2,128)} %broadcast_in_dim.8), calls=%async_computation.3 | async-start | bytes 32768 | tf_op jit(solution)/shard_map/all_to_all | solution.py:205

commit v2 on v1

v2 whole, which is shorter than its diff:
```python
import jax
import jax.numpy as jnp
import numpy as np
from jax import lax
from jax.experimental import pallas as pl
from jax.experimental.pallas import tpu as pltpu
from jax.sharding import PartitionSpec as P


CLASSES = [(pd, ph, pw) for pd in range(2) for ph in range(2) for pw in range(2)]
CHANNELS = 4
FILTERS = 32
TAPS = 27 * CHANNELS
ROWS = 48


def window_shift(pd, ph, pw):
    return ph * 64 + pw * 16 + pd * 4


def tap_table():
    tap = lax.broadcasted_iota(jnp.int32, (128, 256), 0)
    row = lax.broadcasted_iota(jnp.int32, (128, 256), 1)
    j, k, i, c = row >> 6, (row >> 4) & 3, (row >> 2) & 3, row & 3
    inside = (i < 3) & (j < 3) & (k < 3)
    return jnp.where(inside & (tap == (i * 9 + j * 3 + k) * CHANNELS + c), 1.0, 0.0).astype(jnp.bfloat16)


def width_table():
    row = lax.broadcasted_iota(jnp.int32, (256, 512), 0)
    col = lax.broadcasted_iota(jnp.int32, (256, 512), 1)
    same = (row >> 7) == ((col >> 6) & 1)
    return jnp.where(same & ((row & 127) == 2 * (col & 63) - 1 + (col >> 7)), 1.0, 0.0).astype(jnp.bfloat16)


def depth_table(inverse):
    row = lax.broadcasted_iota(jnp.int32, (128, 128), 0)
    col = lax.broadcasted_iota(jnp.int32, (128, 128), 1)
    if inverse:
        row, col = col, row
    return jnp.where(col == (row & 31) * 4 + (row >> 5), 1.0, 0.0).astype(jnp.bfloat16)


def row_table(order):
    table = np.zeros((128, 128), np.float32)
    table[np.arange(128), order] = 1.0
    return table


def forward_kernel(
    vol_ref, low_ref, high_ref, kern_ref, bias_ref, pooled_ref, window, code_ref,
    flat, lines, split, pooled, width
):
    f32, bf16 = jnp.float32, jnp.bfloat16
    width[...] = width_table()
    spread_taps = jnp.dot(kern_ref[...], tap_table(), preferred_element_type=f32)
    weights = jnp.concatenate(
        [
            pltpu.roll(spread_taps, window_shift(*parity), 1) if window_shift(*parity) else spread_taps
            for parity in CLASSES
        ],
        axis=0,
    ).astype(bf16)
    bias = bias_ref[...]
    for c in range(CHANNELS):
        for d in range(10):
            if d == 0:
                plane = low_ref[c, 0]
            elif d == 9:
                plane = high_ref[c, 0]
            else:
                plane = vol_ref[c, d]
            flat[(d * CHANNELS + c) * 32 : (d * CHANNELS + c + 1) * 32, :] = plane.astype(f32)
    zero_line = jnp.zeros((ROWS, 128), bf16)
    lines[0, :, 0:128] = zero_line
    lines[31, :, 128:256] = zero_line
    for h in range(32):
        line = flat[pl.ds(h, 40, stride=32), :]
        line = jnp.concatenate([line, jnp.zeros((8, 128), f32)], axis=0).astype(bf16)
        if h <= 30:
            h4, j = divmod(h + 1, 4)
            lines[j * 8 + h4, :, 0:128] = line
        if h >= 1:
            h4, j = divmod(h - 1, 4)
            lines[j * 8 + h4, :, 128:256] = line
    for j in range(4):
        rows = lines[j * 8 : (j + 1) * 8].reshape(8 * ROWS, 256)
        split[j] = jnp.dot(rows, width[...], preferred_element_type=f32)
    for d2 in range(4):
        for h4 in range(8):
            for j in range(4):
                for k in range(4):
                    first = h4 * ROWS + d2 * 8
                    window[
                        (j * 4 + k) * 16 : (j * 4 + k + 1) * 16,
                        (d2 * 8 + h4) * 128 : (d2 * 8 + h4 + 1) * 128,
                    ] = split[j, first : first + 16, k * 128 : (k + 1) * 128].astype(bf16)

    for d2 in range(4):
        for tile in range(4):
            first = d2 * 1024 + tile * 256
            conv = jnp.dot(weights, window[:, first : first + 256], preferred_element_type=f32)
            for half in range(2):
                lane = tile * 256 + half * 128
                total = jnp.zeros((FILTERS, 128), f32)
                code = jnp.zeros((FILTERS, 128), f32)
                for n in range(8):
                    x = conv[n * FILTERS : (n + 1) * FILTERS, half * 128 : (half + 1) * 128] + bias
                    total = total + jnp.maximum(x, 0.3 * x).astype(bf16).astype(f32)
                    code = code + jnp.where(x > 0, float(1 << n), 0.0)
                code_ref[d2 * FILTERS : (d2 + 1) * FILTERS, lane : lane + 128] = code.astype(bf16)
                pooled[d2 * FILTERS : (d2 + 1) * FILTERS, lane : lane + 128] = (total * 0.125).astype(bf16)
    pooled_ref[...] = jnp.dot(depth_table(True), pooled[...], preferred_element_type=f32).astype(bf16)


def backward_kernel(pooled_ref, window, code_ref, cot_ref, out_ref, spread, cots):
    f32, bf16 = jnp.float32, jnp.bfloat16
    out_ref[:, 0:1024] = pooled_ref[...]
    cots[...] = jnp.dot(depth_table(False), cot_ref[...], preferred_element_type=f32)
    bias_sum = jnp.zeros((FILTERS, 128), f32)
    for d2 in range(4):
        for tile in range(8):
            lane = tile * 128
            first = d2 * 1024 + lane
            incoming = cots[d2 * FILTERS : (d2 + 1) * FILTERS, lane : lane + 128] * 0.125
            full = incoming.astype(bf16).astype(f32)
            part = (incoming * 0.3).astype(bf16).astype(f32)
            code = code_ref[d2 * FILTERS : (d2 + 1) * FILTERS, lane : lane + 128].astype(f32).astype(jnp.int32)
            for n in range(8):
                back = jnp.where((code & (1 << n)) != 0, full, part)
                bias_sum = bias_sum + back
                spread[n * FILTERS : (n + 1) * FILTERS, first : first + 128] = back.astype(bf16)

    grads = lax.dot_general(
        spread[...], window[...], (((1,), (1,)), ((), ())), preferred_element_type=f32
    )
    table = tap_table()
    folded = jnp.zeros((FILTERS, 256), f32)
    for n, parity in enumerate(CLASSES):
        shift = window_shift(*parity)
        block = grads[n * FILTERS : (n + 1) * FILTERS]
        folded = folded + (pltpu.roll(block, 256 - shift, 1) if shift else block)

    def pieces(value):
        one = value.astype(bf16)
        rest = value - one.astype(f32)
        two = rest.astype(bf16)
        three = (rest - two.astype(f32)).astype(bf16)
        return one, two, three

    bias_column = jnp.sum(bias_sum, axis=1, keepdims=True)
    columns = lax.broadcasted_iota(jnp.int32, (FILTERS, 128), 1)
    sent = []
    for taps, own in zip(pieces(folded), pieces(bias_column), strict=True):
        picked = lax.dot_general(taps, table, (((1,), (1,)), ((), ())), preferred_element_type=f32)
        sent.append(jnp.where(columns == TAPS, own.astype(f32), picked))
    sent.append(jnp.zeros((FILTERS, 128), f32))
    stacked = jnp.concatenate(sent, axis=0).astype(bf16)
    out_ref[:, 1024:1152] = jnp.dot(depth_table(True), stacked, preferred_element_type=f32).astype(bf16)


def unpack_kernel(terms_ref, kernel_ref, bias_ref):
    terms = terms_ref[...]
    kernel_ref[...] = terms[:, :TAPS]
    own = lax.broadcasted_iota(jnp.int32, (FILTERS, FILTERS), 0) == lax.broadcasted_iota(
        jnp.int32, (FILTERS, FILTERS), 1
    )
    bias_ref[...] = jnp.sum(jnp.where(own, terms[:, TAPS : TAPS + 1], 0.0), axis=0, keepdims=True)


def in_vmem(kernel, outs, operands, scratch=(), megabytes=24, flops=1_000_000, moved=100_000):
    one = pl.BlockSpec(memory_space=pltpu.VMEM)
    return pl.pallas_call(
        kernel,
        out_shape=outs,
        in_specs=[one] * len(operands),
        out_specs=jax.tree.map(lambda _: one, outs),
        scratch_shapes=list(scratch),
        compiler_params=pltpu.CompilerParams(vmem_limit_bytes=megabytes * 1024 * 1024),
        cost_estimate=pl.CostEstimate(flops=flops, bytes_accessed=moved, transcendentals=0),
    )(*operands)


def reorder(order, rows):
    return jnp.dot(jnp.asarray(row_table(order), rows.dtype), rows, preferred_element_type=rows.dtype)


def on_device(volume, kernel, bias, cotangent):
    f32, bf16 = jnp.float32, jnp.bfloat16
    spaces, batches = lax.axis_size("space"), lax.axis_size("batch")
    owned_rows = np.arange(128).reshape(2, spaces, 4)
    to_slabs = owned_rows.transpose(1, 0, 2).reshape(-1)
    to_owner = np.argsort(to_slabs)
    up = [(i, i + 1) for i in range(spaces - 1)]
    down = [(i + 1, i) for i in range(spaces - 1)]
    local = volume[0]
    low = lax.ppermute(local[:, -1:], "space", up)
    high = lax.ppermute(local[:, :1], "space", down)
    sent = reorder(to_slabs, cotangent.reshape(128, 1024))
    cots = lax.all_to_all(sent, "space", split_axis=0, concat_axis=0, tiled=True)
    slab = jnp.pad(local, ((0, 0), (1, 1), (0, 0), (0, 0)))
    padded = jnp.pad(kernel, ((0, 0), (0, 128 - TAPS)))
    biases = jnp.broadcast_to(bias[:, None], (FILTERS, 128))
    pooled, window, code = in_vmem(
        forward_kernel,
        (
            jax.ShapeDtypeStruct((128, 1024), bf16),
            jax.ShapeDtypeStruct((256, 4096), bf16),
            jax.ShapeDtypeStruct((128, 1024), bf16),
        ),
        (slab, low, high, padded, biases),
        (
            pltpu.VMEM((1280, 128), f32),
            pltpu.VMEM((32, ROWS, 256), bf16),
            pltpu.VMEM((4, 8 * ROWS, 512), f32),
            pltpu.VMEM((128, 1024), bf16),
            pltpu.VMEM((256, 512), bf16),
        ),
        flops=1_000_000_000,
        moved=5_000_000,
    )
    out = in_vmem(
        backward_kernel,
        jax.ShapeDtypeStruct((128, 1152), bf16),
        (pooled, window, code, cots),
        (pltpu.VMEM((256, 4096), bf16), pltpu.VMEM((128, 1024), f32)),
        flops=600_000_000,
        moved=5_000_000,
    )

    out = lax.all_to_all(out, "space", split_axis=0, concat_axis=0, tiled=True)
    pooled = reorder(to_owner, out[:, :1024]).reshape(1, 2, 64, 1024)
    terms = jnp.sum(out[:, 1024:].reshape(spaces, 2, 4, 128).astype(f32), axis=(0, 2))
    terms = lax.all_to_all(
        jnp.broadcast_to(terms[None], (batches, 2, 128)), "batch", split_axis=0, concat_axis=0, tiled=True
    )
    terms = jnp.sum(terms, axis=0)
    terms = lax.all_to_all(
        jnp.broadcast_to(terms[None], (spaces, 2, 128)), "space", split_axis=0, concat_axis=0, tiled=True
    ).reshape(FILTERS, 128)
    kernel_grad, bias_grad = in_vmem(
        unpack_kernel,
        (jax.ShapeDtypeStruct((FILTERS, TAPS), f32), jax.ShapeDtypeStruct((1, FILTERS), f32)),
        (terms,),
        megabytes=4,
    )
    return (pooled, kernel_grad, bias_grad.reshape(FILTERS))


def solution(mesh):
    placed = (P("batch", None, "space", None, None), P(), P(), P("batch", "space", None, None))
    return jax.shard_map(
        on_device,
        mesh=mesh,
        in_specs=placed,
        out_specs=(P("batch", "space", None, None), P(), P()),
        check_vma=False,
    )
```

time: 92.7 us -> 93.4 us (level)
  local copies, waits for them, and re-layouts: 3.03 us -> 4.79 us
  starting transfers between devices: 28.3 us -> 27.1 us
    pad x1 -> x2, local copies, waits for them, and re-layouts: 0.01 us -> 1.69 us  [the longest x1 0.98 us: on_device(): slab = jnp.pad(local, ((0, 0), (1, 1), (0, 0), (0, 0)))]
    pallas_call x1 -> x3, Pallas kernels: 4.61 us -> 5.28 us  [in_vmem(): pl.pallas_call(kernel, out_shape=outs, in_specs=[one] * len(operands), ou...]
  transfers between devices with their start and end apart: 4 -> 4, of which waited for: 2 -> 2; matrix products, arithmetic and copies ran while one was open for 1% -> 4% of each run, Pallas kernels for 0% -> 3%
where the time goes in v2:
time: 93.4 us; the launch traced here: 92.7 us
  blocking collectives  43.6 us (47%)
  starting transfers between devices  27.1 us (29%)
  waiting for transfers between devices  8.54 us (9%)
  Pallas kernels  5.28 us (6%)
  local copies, waits for them, and re-layouts  4.79 us (5%)
  matrix products  2.6 us (3%)
    all_to_all x1, blocking collectives, on_device(): lax.all_to_all(jnp.broadcast_to(terms[None], (batches, 2, 128)), 'batch',...  28.6 us
    all_to_all x1, starting transfers between devices, on_device(): lax.all_to_all(sent, 'space', split_axis=0, concat_axis=0, tiled=True)  18.4 us
    all_to_all x1, blocking collectives, on_device(): out = lax.all_to_all(out, 'space', split_axis=0, concat_axis=0, tiled=True)  15 us
    all_to_all x1, waiting for transfers between devices, on_device(): lax.all_to_all(jnp.broadcast_to(terms[None], (spaces, 2, 128)), 'space',...  6.41 us
    pallas_call x3, Pallas kernels, in_vmem(): pl.pallas_call(kernel, out_shape=outs, in_specs=[one] * len(operands), ou...  5.28 us
    all_to_all x1, starting transfers between devices, on_device(): lax.all_to_all(jnp.broadcast_to(terms[None], (spaces, 2, 128)), 'space',...  4.13 us
    ppermute x1, starting transfers between devices, on_device(): low = lax.ppermute(local[:, -1:], 'space', up)  3.25 us
    dot_general x2, matrix products, reorder(): jnp.dot(jnp.asarray(row_table(order), rows.dtype), rows, preferred_elemen...  2.6 us
  transfers between devices with their start and end apart: 4, of which 2 were waited for; matrix products, arithmetic and copies ran while one was open for 4% of the time, Pallas kernels for 3%

profile of v2, /device:TPU:1, one launch (start us, length us, event | category | flops | bytes accessed | tf_op | source)
XLA Modules:
  0.0 92.7 jit_solution(7346909050170159023)
XLA Ops:
  0.6 0.0 copy-start
  0.6 0.9 %copy-done = bf16[1,2,64,1024]{3,2,1,0:T(8,128)(2,1)S(1)} copy-done((bf16[1,2,64,1024]{3,2,1,0:T(8,128)(2,1)S(1)}, bf16[1,2,64,1024]{3,2,1,0:T(8,128)(2,1)}, u32[]{:S(2)}) %copy-start) | copy-done | bytes 262168
  1.6 1.7 %fusion.3 = bf16[16,8,1024]{2,1,0:T(8,128)(2,1)} fusion(bf16[16,8,128]{2,1,0:T(8,128)(2,1)} %constant.17, bf16[128,1024,1]{1,0,2:T(8,128)(2,1)S(1)} %bitcast.15), kind=kOutput, calls=%fused_computation.4 | convolution fusion | flops 33554432 | bytes 557056 | tf_op jit(solution)/shard_map/dot_general | solution.py:185
  3.3 18.4 %all-to-all-start = ((bf16[16,8,1024]{2,1,0:T(8,128)(2,1)}), bf16[16,8,1024]{2,1,0:T(8,128)(2,1)S(1)}, u32[]{:S(2)}, u32[]{:S(2)}) async-start(bf16[16,8,1024]{2,1,0:T(8,128)(2,1)} %fusion.3), calls=%async_computation | async-start | bytes 524288 | tf_op jit(solution)/shard_map/all_to_all | solution.py:200
  21.7 0.8 fusion.2
  22.5 3.3 %collective-permute-start = (bf16[4,1,32,128]{3,2,1,0:T(8,128)(2,1)S(1)}, bf16[4,1,32,128]{3,2,1,0:T(8,128)(2,1)S(1)}, u32[]{:S(2)}, u32[]{:S(2)}) collective-permute-start(bf16[4,1,32,128]{3,2,1,0:T(8,128)(2,1)S(1)} %get-tuple-element.14), channel_id=1, source_target_pairs={{0,64},{64,128},{128,192},{192,256},{256,320},{320,384},{384,448},... | collective-permute-start | bytes 98312 | tf_op jit(solution)/shard_map/ppermute | solution.py:197
  25.8 1.3 %collective-permute-start.1 = (bf16[4,1,32,128]{3,2,1,0:T(8,128)(2,1)S(1)}, bf16[4,1,32,128]{3,2,1,0:T(8,128)(2,1)S(1)}, u32[]{:S(2)}, u32[]{:S(2)}) collective-permute-start(bf16[4,1,32,128]{3,2,1,0:T(8,128)(2,1)S(1)} %get-tuple-element.13), channel_id=1, source_target_pairs={{64,0},{128,64},{192,128},{256,192},{320,256},{384,320},{448,384},... | collective-permute-start | bytes 98312 | tf_op jit(solution)/shard_map/ppermute | solution.py:198
  27.1 1.0 %pad.8.vol_ref = bf16[4,10,32,128]{3,2,1,0:T(8,128)(2,1)S(1)} pad(bf16[4,8,32,128]{3,2,1,0:T(8,128)(2,1)} %bitcast.22, bf16[]{:T(256)} %constant.3.clone.1), padding=0_0x1_1x0_0x0_0 | pad | bytes 589826 | tf_op jit(solution)/shard_map/jit(_pad)/pad | solution.py:201
  28.1 0.7 pad.9.kern_ref
  28.8 0.0 collective-permute-done.low_ref
  28.8 2.1 %collective-permute-done.1.high_ref = bf16[4,1,32,128]{3,2,1,0:T(8,128)(2,1)S(1)} collective-permute-done((bf16[4,1,32,128]{3,2,1,0:T(8,128)(2,1)S(1)}, bf16[4,1,32,128]{3,2,1,0:T(8,128)(2,1)S(1)}, u32[]{:S(2)}, u32[]{:S(2)}) %collective-permute-start.1) | collective-permute-done | bytes 32800 | tf_op jit(solution)/shard_map/ppermute | solution.py:198
  30.9 0.7 broadcast_in_dim.6.bias_ref
  31.6 2.7 %shard_map.85 = (bf16[128,1024]{1,0:T(8,128)(2,1)S(1)}, bf16[256,4096]{1,0:T(8,128)(2,1)S(1)}, bf16[128,1024]{1,0:T(8,128)(2,1)S(1)}) custom-call(bf16[4,10,32,128]{3,2,1,0:T(8,128)(2,1)S(1)} %pad.8.vol_ref, bf16[4,1,32,128]{3,2,1,0:T(8,128)(2,1)S(1)} %collective-permute-done.low_ref, bf16[4,1,32,128]{3,2,1,0:T(8,128)(2,1)S(1)} %collective-permute-done.1.high_ref, ...), custom_call_target="tpu_custom_call" | custom-call | flops 1000000000 | bytes 5000000 | tf_op jit(solution)/shard_map/pallas_call | solution.py:173
  34.3 0.0 all-to-all-done
  34.3 0.0 copy-start.1
  34.3 2.0 %shard_map.86 = bf16[128,1152]{1,0:T(8,128)(2,1)S(1)} custom-call(bf16[128,1024]{1,0:T(8,128)(2,1)S(1)} %get-tuple-element.8.pooled_ref, bf16[256,4096]{1,0:T(8,128)(2,1)S(1)} %get-tuple-element.9.window, bf16[128,1024]{1,0:T(8,128)(2,1)S(1)} %get-tuple-element.10.code_ref, bf16[128,1024]{1,0:T(8,128)(2,1)S(1)} %bitcast.17), custom_call_target="tpu_custom_call" | custom-call | flops 600000000 | bytes 5000000 | tf_op jit(solution)/shard_map/pallas_call | solution.py:173
  36.3 15.0 %all_to_all.30 = bf16[16,8,1152]{2,1,0:T(8,128)(2,1)S(1)} all-to-all(bf16[16,8,1152]{2,1,0:T(8,128)(2,1)S(1)} %bitcast.16), channel_id=1, replica_groups=mesh['space'=16,'batch'=64] {'space'}, dimensions={0} | all-to-all | bytes 589824 | tf_op jit(solution)/shard_map/all_to_all | solution.py:231
  51.4 28.6 %all_to_all.31 = f32[64,2,128]{2,1,0:T(2,128)S(1)} all-to-all(f32[64,2,128]{2,1,0:T(2,128)S(1)} %broadcast_in_dim.7), channel_id=1, replica_groups=mesh['space'=16,'batch'=64] {'batch'}, dimensions={0} | all-to-all | bytes 131072 | tf_op jit(solution)/shard_map/all_to_all | solution.py:234
  80.0 0.1 reduce_sum.19
  80.0 0.6 broadcast_in_dim.8
  80.7 4.1 %all-to-all-start.3 = ((f32[16,2,128]{2,1,0:T(2,128)}), f32[16,2,128]{2,1,0:T(2,128)S(1)}, u32[]{:S(2)}, u32[]{:S(2)}) async-start(f32[16,2,128]{2,1,0:T(2,128)} %broadcast_in_dim.8), calls=%async_computation.3 | async-start | bytes 32768 | tf_op jit(solution)/shard_map/all_to_all | solution.py:238
  84.8 0.0 copy-done.1
  84.8 0.9 fusion
  85.7 6.4 %all-to-all-done.3 = f32[16,2,128]{2,1,0:T(2,128)S(1)} async-done(((f32[16,2,128]{2,1,0:T(2,128)}), f32[16,2,128]{2,1,0:T(2,128)S(1)}, u32[]{:S(2)}, u32[]{:S(2)}) %all-to-all-start.3) | async-done | bytes 16416 | tf_op jit(solution)/shard_map/all_to_all | solution.py:238
  92.1 0.6 shard_map.87
  (3 shorter events, 0.1 us)
Async XLA Ops:
  0.6 1.0 %copy-start = (bf16[1,2,64,1024]{3,2,1,0:T(8,128)(2,1)S(1)}, bf16[1,2,64,1024]{3,2,1,0:T(8,128)(2,1)}, u32[]{:S(2)}) copy-start(bf16[1,2,64,1024]{3,2,1,0:T(8,128)(2,1)} %param.9) | copy-start | bytes 786436
  3.3 31.0 %all-to-all-start = ((bf16[16,8,1024]{2,1,0:T(8,128)(2,1)}), bf16[16,8,1024]{2,1,0:T(8,128)(2,1)S(1)}, u32[]{:S(2)}, u32[]{:S(2)}) async-start(bf16[16,8,1024]{2,1,0:T(8,128)(2,1)} %fusion.3), calls=%async_computation | async-start | bytes 524288 | tf_op jit(solution)/shard_map/all_to_all | solution.py:200
  22.5 6.3 %collective-permute-start = (bf16[4,1,32,128]{3,2,1,0:T(8,128)(2,1)S(1)}, bf16[4,1,32,128]{3,2,1,0:T(8,128)(2,1)S(1)}, u32[]{:S(2)}, u32[]{:S(2)}) collective-permute-start(bf16[4,1,32,128]{3,2,1,0:T(8,128)(2,1)S(1)} %get-tuple-element.14), channel_id=1, source_target_pairs={{0,64},{64,128},{128,192},{192,256},{256,320},{320,384},{384,448},... | collective-permute-start | bytes 98312 | tf_op jit(solution)/shard_map/ppermute | solution.py:197
  25.8 5.1 %collective-permute-start.1 = (bf16[4,1,32,128]{3,2,1,0:T(8,128)(2,1)S(1)}, bf16[4,1,32,128]{3,2,1,0:T(8,128)(2,1)S(1)}, u32[]{:S(2)}, u32[]{:S(2)}) collective-permute-start(bf16[4,1,32,128]{3,2,1,0:T(8,128)(2,1)S(1)} %get-tuple-element.13), channel_id=1, source_target_pairs={{64,0},{128,64},{192,128},{256,192},{320,256},{384,320},{448,384},... | collective-permute-start | bytes 98312 | tf_op jit(solution)/shard_map/ppermute | solution.py:198
  34.3 50.5 %copy-start.1 = (bf16[128,128]{1,0:T(8,128)(2,1)S(1)}, bf16[128,128]{1,0:T(8,128)(2,1)}, u32[]{:S(2)}) copy-start(bf16[128,128]{1,0:T(8,128)(2,1)} %constant.10.clone) | copy-start | bytes 98308
  80.7 11.5 %all-to-all-start.3 = ((f32[16,2,128]{2,1,0:T(2,128)}), f32[16,2,128]{2,1,0:T(2,128)S(1)}, u32[]{:S(2)}, u32[]{:S(2)}) async-start(f32[16,2,128]{2,1,0:T(2,128)} %broadcast_in_dim.8), calls=%async_computation.3 | async-start | bytes 32768 | tf_op jit(solution)/shard_map/all_to_all | solution.py:238

commit v3 on v2

--- a/solution.py
+++ b/solution.py
@@ -47,13 +47,22 @@
     return table
 
 
-def forward_kernel(
-    vol_ref, low_ref, high_ref, kern_ref, bias_ref, pooled_ref, window, code_ref,
-    flat, lines, split, pooled, width
+def reorder_kernel(rows_ref, last_ref, head_ref, out_ref):
+    row = lax.broadcasted_iota(jnp.int32, (128, 128), 0)
+    col = lax.broadcasted_iota(jnp.int32, (128, 128), 1)
+    table = jnp.where(col == ((row >> 2) & 1) * 64 + (row >> 3) * 4 + (row & 3), 1.0, 0.0).astype(jnp.bfloat16)
+    out_ref[...] = jnp.dot(table, rows_ref[...], preferred_element_type=jnp.float32).astype(jnp.bfloat16)
+
+
+def inner_kernel(
+    vol_ref, columns_ref, pooled_ref, window, code_ref, weights_ref, biases_ref,
+    flat, lines, split, width, padded
 ):
     f32, bf16 = jnp.float32, jnp.bfloat16
     width[...] = width_table()
-    spread_taps = jnp.dot(kern_ref[...], tap_table(), preferred_element_type=f32)
+    padded[...] = jnp.zeros((FILTERS, 128), bf16)
+    padded[:, :TAPS] = columns_ref[:, :TAPS].astype(bf16)
+    spread_taps = jnp.dot(padded[...], tap_table(), preferred_element_type=f32)
     weights = jnp.concatenate(
         [
             pltpu.roll(spread_taps, window_shift(*parity), 1) if window_shift(*parity) else spread_taps
@@ -61,16 +70,15 @@
         ],
         axis=0,
     ).astype(bf16)
-    bias = bias_ref[...]
+    weights_ref[...] = weights
+    bias = jnp.broadcast_to(columns_ref[:, TAPS : TAPS + 1], (FILTERS, 128))
+    biases_ref[...] = bias
+
+    flat[0:128, :] = jnp.zeros((128, 128), f32)
+    flat[1152:1280, :] = jnp.zeros((128, 128), f32)
     for c in range(CHANNELS):
-        for d in range(10):
-            if d == 0:
-                plane = low_ref[c, 0]
-            elif d == 9:
-                plane = high_ref[c, 0]
-            else:
-                plane = vol_ref[c, d]
-            flat[(d * CHANNELS + c) * 32 : (d * CHANNELS + c + 1) * 32, :] = plane.astype(f32)
+        for d in range(1, 9):
+            flat[(d * CHANNELS + c) * 32 : (d * CHANNELS + c + 1) * 32, :] = vol_ref[c, d - 1].astype(f32)
     zero_line = jnp.zeros((ROWS, 128), bf16)
     lines[0, :, 0:128] = zero_line
     lines[31, :, 128:256] = zero_line
@@ -96,9 +104,10 @@
                         (d2 * 8 + h4) * 128 : (d2 * 8 + h4 + 1) * 128,
                     ] = split[j, first : first + 16, k * 128 : (k + 1) * 128].astype(bf16)
 
-    for d2 in range(4):
+    for plane in range(2):
+        rows = slice(plane * FILTERS, (plane + 1) * FILTERS)
         for tile in range(4):
-            first = d2 * 1024 + tile * 256
+            first = (plane + 1) * 1024 + tile * 256
             conv = jnp.dot(weights, window[:, first : first + 256], preferred_element_type=f32)
             for half in range(2):
                 lane = tile * 256 + half * 128
@@ -108,32 +117,94 @@
                     x = conv[n * FILTERS : (n + 1) * FILTERS, half * 128 : (half + 1) * 128] + bias
                     total = total + jnp.maximum(x, 0.3 * x).astype(bf16).astype(f32)
                     code = code + jnp.where(x > 0, float(1 << n), 0.0)
-                code_ref[d2 * FILTERS : (d2 + 1) * FILTERS, lane : lane + 128] = code.astype(bf16)
-                pooled[d2 * FILTERS : (d2 + 1) * FILTERS, lane : lane + 128] = (total * 0.125).astype(bf16)
-    pooled_ref[...] = jnp.dot(depth_table(True), pooled[...], preferred_element_type=f32).astype(bf16)
-
-
-def backward_kernel(pooled_ref, window, code_ref, cot_ref, out_ref, spread, cots):
+                code_ref[rows, lane : lane + 128] = code.astype(bf16)
+                pooled_ref[rows, lane : lane + 128] = (total * 0.125).astype(bf16)
+
+
+def outer_kernel(
+    low_ref, high_ref, cot_ref, inner_ref, window, code_ref, weights_ref, biases_ref, out_ref,
+    flat, lines, split, edge, spread, pooled, cots
+):
     f32, bf16 = jnp.float32, jnp.bfloat16
-    out_ref[:, 0:1024] = pooled_ref[...]
+    for c in range(CHANNELS):
+        flat[c * 32 : (c + 1) * 32, :] = low_ref[c, 0].astype(f32)
+        flat[(CHANNELS + c) * 32 : (CHANNELS + c + 1) * 32, :] = high_ref[c, 0].astype(f32)
+    lines[0, :, 0:128] = jnp.zeros((8, 128), f32)
+    lines[31, :, 128:256] = jnp.zeros((8, 128), f32)
+    for h in range(32):
+        line = flat[pl.ds(h, 8, stride=32), :]
+        if h <= 30:
+            h4, j = divmod(h + 1, 4)
+            lines[j * 8 + h4, :, 0:128] = line
+        if h >= 1:
+            h4, j = divmod(h - 1, 4)
+            lines[j * 8 + h4, :, 128:256] = line
+    split[...] = jnp.dot(lines[...].reshape(256, 256).astype(bf16), width_table(), preferred_element_type=f32)
+
     cots[...] = jnp.dot(depth_table(False), cot_ref[...], preferred_element_type=f32)
+
+    def gradients(d2, lane):
+        incoming = cots[d2 * FILTERS : (d2 + 1) * FILTERS, lane : lane + 128] * 0.125
+        return incoming.astype(bf16).astype(f32), (incoming * 0.3).astype(bf16).astype(f32)
+
     bias_sum = jnp.zeros((FILTERS, 128), f32)
-    for d2 in range(4):
+    for plane in range(2):
+        rows = slice((plane + 1) * FILTERS, (plane + 2) * FILTERS)
+        held = slice(plane * FILTERS, (plane + 1) * FILTERS)
+        pooled[rows, :] = inner_ref[held, :]
         for tile in range(8):
             lane = tile * 128
-            first = d2 * 1024 + lane
-            incoming = cots[d2 * FILTERS : (d2 + 1) * FILTERS, lane : lane + 128] * 0.125
-            full = incoming.astype(bf16).astype(f32)
-            part = (incoming * 0.3).astype(bf16).astype(f32)
-            code = code_ref[d2 * FILTERS : (d2 + 1) * FILTERS, lane : lane + 128].astype(f32).astype(jnp.int32)
+            first = (plane + 1) * 1024 + lane
+            full, part = gradients(plane + 1, lane)
+            code = code_ref[held, lane : lane + 128].astype(f32).astype(jnp.int32)
             for n in range(8):
                 back = jnp.where((code & (1 << n)) != 0, full, part)
                 bias_sum = bias_sum + back
                 spread[n * FILTERS : (n + 1) * FILTERS, first : first + 128] = back.astype(bf16)
-
     grads = lax.dot_general(
-        spread[...], window[...], (((1,), (1,)), ((), ())), preferred_element_type=f32
-    )
+        spread[:, 1024:3072], window[:, 1024:3072], (((1,), (1,)), ((), ())), preferred_element_type=f32
+    )
+
+    sublane = lax.broadcasted_iota(jnp.int32, (8, 128), 0)
+    nothing = jnp.zeros((8, 128), f32)
+    bias = biases_ref[...]
+    for side in range(2):
+        d2 = 3 * side
+        for h4 in range(8):
+            for j in range(4):
+                for k in range(4):
+                    rows = slice((j * 4 + k) * 16, (j * 4 + k + 1) * 16)
+                    new = split[(j * 8 + h4) * 8 : (j * 8 + h4 + 1) * 8, k * 128 : (k + 1) * 128]
+                    if side == 0:
+                        new = jnp.concatenate([jnp.where(sublane < 4, new, 0.0), nothing], axis=0)
+                    else:
+                        new = jnp.concatenate([nothing, jnp.where(sublane < 4, 0.0, new)], axis=0)
+                    own = window[rows, (d2 * 8 + h4) * 128 : (d2 * 8 + h4 + 1) * 128]
+                    edge[rows, (side * 8 + h4) * 128 : (side * 8 + h4 + 1) * 128] = own + new.astype(bf16)
+        for tile in range(4):
+            first = side * 1024 + tile * 256
+            conv = jnp.dot(weights_ref[...], edge[:, first : first + 256], preferred_element_type=f32)
+            for half in range(2):
+                lane = tile * 256 + half * 128
+                full, part = gradients(d2, lane)
+                total = jnp.zeros((FILTERS, 128), f32)
+                for n in range(8):
+                    x = conv[n * FILTERS : (n + 1) * FILTERS, half * 128 : (half + 1) * 128] + bias
+                    total = total + jnp.maximum(x, 0.3 * x).astype(bf16).astype(f32)
+                    back = jnp.where(x > 0, full, part)
+                    bias_sum = bias_sum + back
+                    spread[
+                        n * FILTERS : (n + 1) * FILTERS, d2 * 1024 + lane : d2 * 1024 + lane + 128
+                    ] = back.astype(bf16)
+                pooled[d2 * FILTERS : (d2 + 1) * FILTERS, lane : lane + 128] = (total * 0.125).astype(bf16)
+        grads = grads + lax.dot_general(
+            spread[:, d2 * 1024 : (d2 + 1) * 1024],
+            edge[:, side * 1024 : (side + 1) * 1024],
+            (((1,), (1,)), ((), ())),
+            preferred_element_type=f32,
+        )
+    out_ref[:, 0:1024] = jnp.dot(depth_table(True), pooled[...], preferred_element_type=f32).astype(bf16)
+
     table = tap_table()
     folded = jnp.zeros((FILTERS, 256), f32)
     for n, parity in enumerate(CLASSES):
@@ -194,36 +265,51 @@
     up = [(i, i + 1) for i in range(spaces - 1)]
     down = [(i + 1, i) for i in range(spaces - 1)]
     local = volume[0]
-    low = lax.ppermute(local[:, -1:], "space", up)
-    high = lax.ppermute(local[:, :1], "space", down)
-    sent = reorder(to_slabs, cotangent.reshape(128, 1024))
+    last, head = lax.optimization_barrier((local[:, -1:], local[:, :1]))
+    sent = in_vmem(
+        reorder_kernel,
+        jax.ShapeDtypeStruct((128, 1024), bf16),
+        (cotangent.reshape(128, 1024), last, head),
+        megabytes=4,
+    )
     cots = lax.all_to_all(sent, "space", split_axis=0, concat_axis=0, tiled=True)
-    slab = jnp.pad(local, ((0, 0), (1, 1), (0, 0), (0, 0)))
-    padded = jnp.pad(kernel, ((0, 0), (0, 128 - TAPS)))
-    biases = jnp.broadcast_to(bias[:, None], (FILTERS, 128))
-    pooled, window, code = in_vmem(
-        forward_kernel,
-        (
-            jax.ShapeDtypeStruct((128, 1024), bf16),
-            jax.ShapeDtypeStruct((256, 4096), bf16),
-            jax.ShapeDtypeStruct((128, 1024), bf16),
-        ),
-        (slab, low, high, padded, biases),
+    low = lax.ppermute(last, "space", up)
+    high = lax.ppermute(head, "space", down)
+    columns = jnp.concatenate([kernel.astype(f32), bias[:, None]], axis=1)
+    shapes = (
+        jax.ShapeDtypeStruct((64, 1024), bf16),
+        jax.ShapeDtypeStruct((256, 4096), bf16),
+        jax.ShapeDtypeStruct((64, 1024), bf16),
+        jax.ShapeDtypeStruct((256, 256), bf16),
+        jax.ShapeDtypeStruct((FILTERS, 128), f32),
+    )
+    inner = in_vmem(
+        inner_kernel,
+        shapes,
+        (local, columns),
         (
             pltpu.VMEM((1280, 128), f32),
             pltpu.VMEM((32, ROWS, 256), bf16),
             pltpu.VMEM((4, 8 * ROWS, 512), f32),
-            pltpu.VMEM((128, 1024), bf16),
             pltpu.VMEM((256, 512), bf16),
+            pltpu.VMEM((FILTERS, 128), bf16),
         ),
         flops=1_000_000_000,
         moved=5_000_000,
     )
     out = in_vmem(
-        backward_kernel,
+        outer_kernel,
         jax.ShapeDtypeStruct((128, 1152), bf16),
-        (pooled, window, code, cots),
-        (pltpu.VMEM((256, 4096), bf16), pltpu.VMEM((128, 1024), f32)),
+        (low, high, cots, *inner),
+        (
+            pltpu.VMEM((256, 128), f32),
+            pltpu.VMEM((32, 8, 256), f32),
+            pltpu.VMEM((256, 512), f32),
+            pltpu.VMEM((256, 2048), bf16),
+            pltpu.VMEM((256, 4096), bf16),
+            pltpu.VMEM((128, 1024), bf16),
+            pltpu.VMEM((128, 1024), f32),
+        ),
         flops=600_000_000,
         moved=5_000_000,
     )

time: 93.4 us -> 92.5 us (level)
  blocking collectives: 43.6 us -> 45.7 us
  waiting for transfers between devices: 8.54 us -> 6.5 us
  matrix products: 2.6 us -> 0.92 us
    all_to_all x1, blocking collectives: 15 us -> 17.2 us  [on_device(): out = lax.all_to_all(out, 'space', split_axis=0, concat_axis=0, tiled=True)]
    ppermute x2, waiting for transfers between devices: 2.12 us -> 0.09 us  [the longest x1 0.08 us: on_device(): high = lax.ppermute(head, 'space', down)]
    pad x2 -> x0, local copies, waits for them, and re-layouts: 1.69 us -> none  [the longest x1 0.98 us: on_device(): slab = jnp.pad(local, ((0, 0), (1, 1), (0, 0), (0, 0)))]
    dot_general x2 -> x1, matrix products: 2.6 us -> 0.92 us  [reorder(): jnp.dot(jnp.asarray(row_table(order), rows.dtype), rows, preferred_elemen...]
    unnamed x4 -> x6, local copies, waits for them, and re-layouts: 0.96 us -> 1.91 us
    pallas_call x3 -> x4, Pallas kernels: 5.28 us -> 6.21 us  [in_vmem(): pl.pallas_call(kernel, out_shape=outs, in_specs=[one] * len(operands), ou...]
  transfers between devices with their start and end apart: 4 -> 4, of which waited for: 2 -> 2; matrix products, arithmetic and copies ran while one was open for 4% -> 3% of each run, Pallas kernels for 3% -> 2%
where the time goes in v3:
time: 92.5 us; the launch traced here: 92 us
  blocking collectives  45.7 us (49%)
  starting transfers between devices  27 us (29%)
  waiting for transfers between devices  6.5 us (7%)
  Pallas kernels  6.21 us (7%)
  local copies, waits for them, and re-layouts  4.07 us (4%)
    all_to_all x1, blocking collectives, on_device(): lax.all_to_all(jnp.broadcast_to(terms[None], (batches, 2, 128)), 'batch',...  28.5 us
    all_to_all x1, starting transfers between devices, on_device(): lax.all_to_all(sent, 'space', split_axis=0, concat_axis=0, tiled=True)  18.5 us
    all_to_all x1, blocking collectives, on_device(): out = lax.all_to_all(out, 'space', split_axis=0, concat_axis=0, tiled=True)  17.2 us
    all_to_all x1, waiting for transfers between devices, on_device(): lax.all_to_all(jnp.broadcast_to(terms[None], (spaces, 2, 128)), 'space',...  6.41 us
    pallas_call x4, Pallas kernels, in_vmem(): pl.pallas_call(kernel, out_shape=outs, in_specs=[one] * len(operands), ou...  6.21 us
    all_to_all x1, starting transfers between devices, on_device(): lax.all_to_all(jnp.broadcast_to(terms[None], (spaces, 2, 128)), 'space',...  3.96 us
    ppermute x1, starting transfers between devices, on_device(): low = lax.ppermute(last, 'space', up)  3.26 us
    unnamed x6, local copies, waits for them, and re-layouts  1.91 us
  transfers between devices with their start and end apart: 4, of which 2 were waited for; matrix products, arithmetic and copies ran while one was open for 3% of the time, Pallas kernels for 2%

profile of v3, /device:TPU:1, one launch (start us, length us, event | category | flops | bytes accessed | tf_op | source)
XLA Modules:
  0.0 92.0 jit_solution(15571256580744599868)
XLA Ops:
  0.6 0.8 fusion.2
  1.4 0.0 copy-start
  1.4 0.9 %copy-done = bf16[1,2,64,1024]{3,2,1,0:T(8,128)(2,1)S(1)} copy-done((bf16[1,2,64,1024]{3,2,1,0:T(8,128)(2,1)S(1)}, bf16[1,2,64,1024]{3,2,1,0:T(8,128)(2,1)}, u32[]{:S(2)}) %copy-start) | copy-done | bytes 262168
  2.4 0.9 shard_map.76
  3.3 18.5 %all-to-all-start = ((bf16[16,8,1024]{2,1,0:T(8,128)(2,1)}), bf16[16,8,1024]{2,1,0:T(8,128)(2,1)S(1)}, u32[]{:S(2)}, u32[]{:S(2)}) async-start(bf16[16,8,1024]{2,1,0:T(8,128)(2,1)} %bitcast.2), calls=%async_computation | async-start | bytes 524288 | tf_op jit(solution)/shard_map/all_to_all | solution.py:275
  21.7 3.3 %collective-permute-start = (bf16[4,1,32,128]{3,2,1,0:T(8,128)(2,1)S(1)}, bf16[4,1,32,128]{3,2,1,0:T(8,128)(2,1)S(1)}, u32[]{:S(2)}, u32[]{:S(2)}) collective-permute-start(bf16[4,1,32,128]{3,2,1,0:T(8,128)(2,1)S(1)} %get-tuple-element.12.last_ref), channel_id=1, source_target_pairs={{0,64},{64,128},{128,192},{192,256},{256,320},{320,384},{384,448},... | collective-permute-start | bytes 98312 | tf_op jit(solution)/shard_map/ppermute | solution.py:276
  25.0 1.3 %collective-permute-start.1 = (bf16[4,1,32,128]{3,2,1,0:T(8,128)(2,1)S(1)}, bf16[4,1,32,128]{3,2,1,0:T(8,128)(2,1)S(1)}, u32[]{:S(2)}, u32[]{:S(2)}) collective-permute-start(bf16[4,1,32,128]{3,2,1,0:T(8,128)(2,1)S(1)} %get-tuple-element.13.head_ref), channel_id=1, source_target_pairs={{64,0},{128,64},{192,128},{256,192},{320,256},{384,320},{448,384},... | collective-permute-start | bytes 98312 | tf_op jit(solution)/shard_map/ppermute | solution.py:277
  26.3 0.7 convert_element_type.9
  27.0 0.7 copy.10
  27.7 0.1 pad_maximum_fusion.columns_ref
  27.8 0.0 copy-start.1
  27.8 0.9 %copy-done.1 = bf16[1,4,8,32,128]{4,3,2,1,0:T(8,128)(2,1)S(1)} copy-done((bf16[1,4,8,32,128]{4,3,2,1,0:T(8,128)(2,1)S(1)}, bf16[1,4,8,32,128]{4,3,2,1,0:T(8,128)(2,1)}, u32[]{:S(2)}) %copy-start.1) | copy-done | bytes 262168
  28.8 1.8 %shard_map.77 = (bf16[64,1024]{1,0:T(8,128)(2,1)S(1)}, bf16[256,4096]{1,0:T(8,128)(2,1)S(1)}, bf16[64,1024]{1,0:T(8,128)(2,1)S(1)}, bf16[256,256]{1,0:T(8,128)(2,1)S(1)}, f32[32,128]{1,0:T(8,128)S(1)}) custom-call(bf16[4,8,32,128]{3,2,1,0:T(8,128)(2,1)S(1)} %bitcast.18, f32[32,109]{1,0:T(8,128)S(1)} %pad_maximum_fusion.columns_ref), custom_call_target="tpu_custom_call" | custom-call | flops 1000000000 | bytes 5000000 | tf_op jit(solution)/shard_map/pallas_call | solution.py:244
  30.6 0.0 copy-start.2
  30.6 0.0 collective-permute-done.low_ref
  30.6 0.1 collective-permute-done.1.high_ref
  30.7 0.0 all-to-all-done
  30.7 2.9 %shard_map.78 = bf16[128,1152]{1,0:T(8,128)(2,1)S(1)} custom-call(bf16[4,1,32,128]{3,2,1,0:T(8,128)(2,1)S(1)} %collective-permute-done.low_ref, bf16[4,1,32,128]{3,2,1,0:T(8,128)(2,1)S(1)} %collective-permute-done.1.high_ref, bf16[128,1024]{1,0:T(8,128)(2,1)S(1)} %bitcast.14, bf16[64,1024]{1,0:T(8,128)(2,1)S(1)} %get-tuple-element.14.inner_ref, ...), custom_call_target="tpu_custom_call" | custom-call | flops 600000000 | bytes 5000000 | tf_op jit(solution)/shard_map/pallas_call | solution.py:244
  33.6 17.2 %all_to_all.33 = bf16[16,8,1152]{2,1,0:T(8,128)(2,1)S(1)} all-to-all(bf16[16,8,1152]{2,1,0:T(8,128)(2,1)S(1)} %bitcast.13), channel_id=1, replica_groups=mesh['space'=16,'batch'=64] {'space'}, dimensions={0} | all-to-all | bytes 589824 | tf_op jit(solution)/shard_map/all_to_all | solution.py:317
  50.8 28.5 %all_to_all.34 = f32[64,2,128]{2,1,0:T(2,128)S(1)} all-to-all(f32[64,2,128]{2,1,0:T(2,128)S(1)} %broadcast_in_dim.7), channel_id=1, replica_groups=mesh['space'=16,'batch'=64] {'batch'}, dimensions={0} | all-to-all | bytes 131072 | tf_op jit(solution)/shard_map/all_to_all | solution.py:320
  79.3 0.1 reduce_sum.19
  79.4 0.6 broadcast_in_dim.8
  80.0 4.0 %all-to-all-start.3 = ((f32[16,2,128]{2,1,0:T(2,128)}), f32[16,2,128]{2,1,0:T(2,128)S(1)}, u32[]{:S(2)}, u32[]{:S(2)}) async-start(f32[16,2,128]{2,1,0:T(2,128)} %broadcast_in_dim.8), calls=%async_computation.3 | async-start | bytes 32768 | tf_op jit(solution)/shard_map/all_to_all | solution.py:324
  84.0 0.0 copy-done.2
  84.0 0.9 fusion
  84.9 6.4 %all-to-all-done.3 = f32[16,2,128]{2,1,0:T(2,128)S(1)} async-done(((f32[16,2,128]{2,1,0:T(2,128)}), f32[16,2,128]{2,1,0:T(2,128)S(1)}, u32[]{:S(2)}, u32[]{:S(2)}) %all-to-all-start.3) | async-done | bytes 16416 | tf_op jit(solution)/shard_map/all_to_all | solution.py:324
  91.3 0.6 shard_map.79
  (3 shorter events, 0.1 us)
Async XLA Ops:
  1.4 0.9 %copy-start = (bf16[1,2,64,1024]{3,2,1,0:T(8,128)(2,1)S(1)}, bf16[1,2,64,1024]{3,2,1,0:T(8,128)(2,1)}, u32[]{:S(2)}) copy-start(bf16[1,2,64,1024]{3,2,1,0:T(8,128)(2,1)} %param.8) | copy-start | bytes 786436
  3.3 27.4 %all-to-all-start = ((bf16[16,8,1024]{2,1,0:T(8,128)(2,1)}), bf16[16,8,1024]{2,1,0:T(8,128)(2,1)S(1)}, u32[]{:S(2)}, u32[]{:S(2)}) async-start(bf16[16,8,1024]{2,1,0:T(8,128)(2,1)} %bitcast.2), calls=%async_computation | async-start | bytes 524288 | tf_op jit(solution)/shard_map/all_to_all | solution.py:275
  21.7 8.9 %collective-permute-start = (bf16[4,1,32,128]{3,2,1,0:T(8,128)(2,1)S(1)}, bf16[4,1,32,128]{3,2,1,0:T(8,128)(2,1)S(1)}, u32[]{:S(2)}, u32[]{:S(2)}) collective-permute-start(bf16[4,1,32,128]{3,2,1,0:T(8,128)(2,1)S(1)} %get-tuple-element.12.last_ref), channel_id=1, source_target_pairs={{0,64},{64,128},{128,192},{192,256},{256,320},{320,384},{384,448},... | collective-permute-start | bytes 98312 | tf_op jit(solution)/shard_map/ppermute | solution.py:276
  25.0 5.7 %collective-permute-start.1 = (bf16[4,1,32,128]{3,2,1,0:T(8,128)(2,1)S(1)}, bf16[4,1,32,128]{3,2,1,0:T(8,128)(2,1)S(1)}, u32[]{:S(2)}, u32[]{:S(2)}) collective-permute-start(bf16[4,1,32,128]{3,2,1,0:T(8,128)(2,1)S(1)} %get-tuple-element.13.head_ref), channel_id=1, source_target_pairs={{64,0},{128,64},{192,128},{256,192},{320,256},{384,320},{448,384},... | collective-permute-start | bytes 98312 | tf_op jit(solution)/shard_map/ppermute | solution.py:277
  27.8 1.0 %copy-start.1 = (bf16[1,4,8,32,128]{4,3,2,1,0:T(8,128)(2,1)S(1)}, bf16[1,4,8,32,128]{4,3,2,1,0:T(8,128)(2,1)}, u32[]{:S(2)}) copy-start(bf16[1,4,8,32,128]{4,3,2,1,0:T(8,128)(2,1)} %param.5) | copy-start | bytes 786436
  30.6 53.4 %copy-start.2 = (bf16[128,128]{1,0:T(8,128)(2,1)S(1)}, bf16[128,128]{1,0:T(8,128)(2,1)}, u32[]{:S(2)}) copy-start(bf16[128,128]{1,0:T(8,128)(2,1)} %constant.4.clone) | copy-start | bytes 98308
  80.0 11.3 %all-to-all-start.3 = ((f32[16,2,128]{2,1,0:T(2,128)}), f32[16,2,128]{2,1,0:T(2,128)S(1)}, u32[]{:S(2)}, u32[]{:S(2)}) async-start(f32[16,2,128]{2,1,0:T(2,128)} %broadcast_in_dim.8), calls=%async_computation.3 | async-start | bytes 32768 | tf_op jit(solution)/shard_map/all_to_all | solution.py:324

commit v4 on v3

--- a/solution.py
+++ b/solution.py
@@ -275,7 +275,9 @@
     cots = lax.all_to_all(sent, "space", split_axis=0, concat_axis=0, tiled=True)
     low = lax.ppermute(last, "space", up)
     high = lax.ppermute(head, "space", down)
-    columns = jnp.concatenate([kernel.astype(f32), bias[:, None]], axis=1)
+    wide = jnp.pad(kernel, ((0, 0), (0, 128 - TAPS))).astype(f32)
+    column = lax.broadcasted_iota(jnp.int32, (FILTERS, 128), 1)
+    columns = jnp.where(column == TAPS, lax.broadcast_in_dim(bias, (FILTERS, 128), (0,)), wide)
     shapes = (
         jax.ShapeDtypeStruct((64, 1024), bf16),
         jax.ShapeDtypeStruct((256, 4096), bf16),
@@ -317,10 +319,16 @@
     out = lax.all_to_all(out, "space", split_axis=0, concat_axis=0, tiled=True)
     pooled = reorder(to_owner, out[:, :1024]).reshape(1, 2, 64, 1024)
     terms = jnp.sum(out[:, 1024:].reshape(spaces, 2, 4, 128).astype(f32), axis=(0, 2))
-    terms = lax.all_to_all(
-        jnp.broadcast_to(terms[None], (batches, 2, 128)), "batch", split_axis=0, concat_axis=0, tiled=True
-    )
-    terms = jnp.sum(terms, axis=0)
+    fine = 8
+    coarse = batches // fine
+    far = [[i + fine * k for k in range(coarse)] for i in range(fine)]
+    near = [[fine * k + i for i in range(fine)] for k in range(coarse)]
+    for groups in (far, near):
+        copies = jnp.broadcast_to(terms[None], (len(groups[0]), 2, 128))
+        terms = jnp.sum(
+            lax.all_to_all(copies, "batch", split_axis=0, concat_axis=0, axis_index_groups=groups, tiled=True),
+            axis=0,
+        )
     terms = lax.all_to_all(
         jnp.broadcast_to(terms[None], (spaces, 2, 128)), "space", split_axis=0, concat_axis=0, tiled=True
     ).reshape(FILTERS, 128)

time: 92.5 us -> 95.1 us (1.028)
  blocking collectives: 45.7 us -> 48.3 us
    all_to_all x1 -> x2, blocking collectives: 28.5 us -> 31.9 us  [on_device(): lax.all_to_all(copies, 'batch', split_axis=0, concat_axis=0, axis_index_g...]
  transfers between devices with their start and end apart: 4 -> 4, of which waited for: 2 -> 2; matrix products, arithmetic and copies ran while one was open for 3% -> 2% of each run, Pallas kernels for 2% -> 2%
where the time goes in v4:
time: 95.1 us; the launch traced here: 94.5 us
  blocking collectives  48.3 us (51%)
  starting transfers between devices  27 us (28%)
  waiting for transfers between devices  7.23 us (8%)
  Pallas kernels  6.21 us (7%)
  local copies, waits for them, and re-layouts  3.32 us (3%)
    all_to_all x2, blocking collectives, on_device(): lax.all_to_all(copies, 'batch', split_axis=0, concat_axis=0, axis_index_g...  31.9 us
    all_to_all x1, starting transfers between devices, on_device(): lax.all_to_all(sent, 'space', split_axis=0, concat_axis=0, tiled=True)  18.5 us
    all_to_all x1, blocking collectives, on_device(): out = lax.all_to_all(out, 'space', split_axis=0, concat_axis=0, tiled=True)  16.4 us
    all_to_all x1, waiting for transfers between devices, on_device(): lax.all_to_all(jnp.broadcast_to(terms[None], (spaces, 2, 128)), 'space',...  6.41 us
    pallas_call x4, Pallas kernels, in_vmem(): pl.pallas_call(kernel, out_shape=outs, in_specs=[one] * len(operands), ou...  6.21 us
    all_to_all x1, starting transfers between devices, on_device(): lax.all_to_all(jnp.broadcast_to(terms[None], (spaces, 2, 128)), 'space',...  3.96 us
    ppermute x1, starting transfers between devices, on_device(): low = lax.ppermute(last, 'space', up)  3.26 us
    unnamed x6, local copies, waits for them, and re-layouts  1.91 us
  transfers between devices with their start and end apart: 4, of which 2 were waited for; matrix products, arithmetic and copies ran while one was open for 2% of the time, Pallas kernels for 2%

profile of v4, /device:TPU:1, one launch (start us, length us, event | category | flops | bytes accessed | tf_op | source)
XLA Modules:
  0.0 94.5 jit_solution(12796373086813247419)
XLA Ops:
  0.6 0.8 fusion.2
  1.4 0.0 copy-start
  1.4 0.9 %copy-done = bf16[1,2,64,1024]{3,2,1,0:T(8,128)(2,1)S(1)} copy-done((bf16[1,2,64,1024]{3,2,1,0:T(8,128)(2,1)S(1)}, bf16[1,2,64,1024]{3,2,1,0:T(8,128)(2,1)}, u32[]{:S(2)}) %copy-start) | copy-done | bytes 262168
  2.4 0.9 shard_map.76
  3.3 18.5 %all-to-all-start = ((bf16[16,8,1024]{2,1,0:T(8,128)(2,1)}), bf16[16,8,1024]{2,1,0:T(8,128)(2,1)S(1)}, u32[]{:S(2)}, u32[]{:S(2)}) async-start(bf16[16,8,1024]{2,1,0:T(8,128)(2,1)} %bitcast.2), calls=%async_computation | async-start | bytes 524288 | tf_op jit(solution)/shard_map/all_to_all | solution.py:275
  21.7 3.3 %collective-permute-start = (bf16[4,1,32,128]{3,2,1,0:T(8,128)(2,1)S(1)}, bf16[4,1,32,128]{3,2,1,0:T(8,128)(2,1)S(1)}, u32[]{:S(2)}, u32[]{:S(2)}) collective-permute-start(bf16[4,1,32,128]{3,2,1,0:T(8,128)(2,1)S(1)} %get-tuple-element.12.last_ref), channel_id=1, source_target_pairs={{0,64},{64,128},{128,192},{192,256},{256,320},{320,384},{384,448},... | collective-permute-start | bytes 98312 | tf_op jit(solution)/shard_map/ppermute | solution.py:276
  25.0 1.3 %collective-permute-start.1 = (bf16[4,1,32,128]{3,2,1,0:T(8,128)(2,1)S(1)}, bf16[4,1,32,128]{3,2,1,0:T(8,128)(2,1)S(1)}, u32[]{:S(2)}, u32[]{:S(2)}) collective-permute-start(bf16[4,1,32,128]{3,2,1,0:T(8,128)(2,1)S(1)} %get-tuple-element.13.head_ref), channel_id=1, source_target_pairs={{64,0},{128,64},{192,128},{256,192},{320,256},{384,320},{448,384},... | collective-permute-start | bytes 98312 | tf_op jit(solution)/shard_map/ppermute | solution.py:277
  26.3 0.8 convert_select_fusion.columns_ref
  27.1 0.0 copy-start.1
  27.1 0.9 %copy-done.1 = bf16[1,4,8,32,128]{4,3,2,1,0:T(8,128)(2,1)S(1)} copy-done((bf16[1,4,8,32,128]{4,3,2,1,0:T(8,128)(2,1)S(1)}, bf16[1,4,8,32,128]{4,3,2,1,0:T(8,128)(2,1)}, u32[]{:S(2)}) %copy-start.1) | copy-done | bytes 262168
  28.0 1.8 %shard_map.77 = (bf16[64,1024]{1,0:T(8,128)(2,1)S(1)}, bf16[256,4096]{1,0:T(8,128)(2,1)S(1)}, bf16[64,1024]{1,0:T(8,128)(2,1)S(1)}, bf16[256,256]{1,0:T(8,128)(2,1)S(1)}, f32[32,128]{1,0:T(8,128)S(1)}) custom-call(bf16[4,8,32,128]{3,2,1,0:T(8,128)(2,1)S(1)} %bitcast.17, f32[32,128]{1,0:T(8,128)S(1)} %convert_select_fusion.columns_ref), custom_call_target="tpu_custom_call" | custom-call | flops 1000000000 | bytes 5000000 | tf_op jit(solution)/shard_map/pallas_call | solution.py:244
  29.9 0.0 copy-start.2
  29.9 0.0 collective-permute-done.low_ref
  29.9 0.8 collective-permute-done.1.high_ref
  30.7 0.0 all-to-all-done
  30.7 2.9 %shard_map.78 = bf16[128,1152]{1,0:T(8,128)(2,1)S(1)} custom-call(bf16[4,1,32,128]{3,2,1,0:T(8,128)(2,1)S(1)} %collective-permute-done.low_ref, bf16[4,1,32,128]{3,2,1,0:T(8,128)(2,1)S(1)} %collective-permute-done.1.high_ref, bf16[128,1024]{1,0:T(8,128)(2,1)S(1)} %bitcast.13, bf16[64,1024]{1,0:T(8,128)(2,1)S(1)} %get-tuple-element.14.inner_ref, ...), custom_call_target="tpu_custom_call" | custom-call | flops 600000000 | bytes 5000000 | tf_op jit(solution)/shard_map/pallas_call | solution.py:244
  33.6 16.4 %all_to_all.38 = bf16[16,8,1152]{2,1,0:T(8,128)(2,1)S(1)} all-to-all(bf16[16,8,1152]{2,1,0:T(8,128)(2,1)S(1)} %bitcast.12), channel_id=1, replica_groups=mesh['space'=16,'batch'=64] {'space'}, dimensions={0} | all-to-all | bytes 589824 | tf_op jit(solution)/shard_map/all_to_all | solution.py:319
  50.1 12.9 %all_to_all.39 = f32[8,2,128]{2,1,0:T(2,128)S(1)} all-to-all(f32[8,2,128]{2,1,0:T(2,128)S(1)} %broadcast_in_dim.9), channel_id=1, replica_groups={{0,8,16,24,32,40,48,56},{1,9,17,25,33,41,49,57},{2,10,18,26,34,42,50,58..., dimensions={0} | all-to-all | bytes 16384 | tf_op jit(solution)/shard_map/all_to_all | solution.py:329
  63.0 19.0 %all_to_all.40 = f32[8,2,128]{2,1,0:T(2,128)S(1)} all-to-all(f32[8,2,128]{2,1,0:T(2,128)S(1)} %broadcast_in_dim.10), channel_id=1, replica_groups={{0,1,2,3,4,5,6,7},{8,9,10,11,12,13,14,15},{16,17,18,19,20,21,22,23},{24..., dimensions={0} | all-to-all | bytes 16384 | tf_op jit(solution)/shard_map/all_to_all | solution.py:329
  82.0 0.6 broadcast_in_dim.11
  82.6 4.0 %all-to-all-start.4 = ((f32[16,2,128]{2,1,0:T(2,128)}), f32[16,2,128]{2,1,0:T(2,128)S(1)}, u32[]{:S(2)}, u32[]{:S(2)}) async-start(f32[16,2,128]{2,1,0:T(2,128)} %broadcast_in_dim.11), calls=%async_computation.4 | async-start | bytes 32768 | tf_op jit(solution)/shard_map/all_to_all | solution.py:332
  86.6 0.0 copy-done.2
  86.6 0.9 fusion
  87.5 6.4 %all-to-all-done.4 = f32[16,2,128]{2,1,0:T(2,128)S(1)} async-done(((f32[16,2,128]{2,1,0:T(2,128)}), f32[16,2,128]{2,1,0:T(2,128)S(1)}, u32[]{:S(2)}, u32[]{:S(2)}) %all-to-all-start.4) | async-done | bytes 16416 | tf_op jit(solution)/shard_map/all_to_all | solution.py:332
  93.9 0.6 shard_map.79
  (7 shorter events, 0.1 us)
Async XLA Ops:
  1.4 0.9 %copy-start = (bf16[1,2,64,1024]{3,2,1,0:T(8,128)(2,1)S(1)}, bf16[1,2,64,1024]{3,2,1,0:T(8,128)(2,1)}, u32[]{:S(2)}) copy-start(bf16[1,2,64,1024]{3,2,1,0:T(8,128)(2,1)} %param.8) | copy-start | bytes 786436
  3.3 27.4 %all-to-all-start = ((bf16[16,8,1024]{2,1,0:T(8,128)(2,1)}), bf16[16,8,1024]{2,1,0:T(8,128)(2,1)S(1)}, u32[]{:S(2)}, u32[]{:S(2)}) async-start(bf16[16,8,1024]{2,1,0:T(8,128)(2,1)} %bitcast.2), calls=%async_computation | async-start | bytes 524288 | tf_op jit(solution)/shard_map/all_to_all | solution.py:275
  21.7 8.2 %collective-permute-start = (bf16[4,1,32,128]{3,2,1,0:T(8,128)(2,1)S(1)}, bf16[4,1,32,128]{3,2,1,0:T(8,128)(2,1)S(1)}, u32[]{:S(2)}, u32[]{:S(2)}) collective-permute-start(bf16[4,1,32,128]{3,2,1,0:T(8,128)(2,1)S(1)} %get-tuple-element.12.last_ref), channel_id=1, source_target_pairs={{0,64},{64,128},{128,192},{192,256},{256,320},{320,384},{384,448},... | collective-permute-start | bytes 98312 | tf_op jit(solution)/shard_map/ppermute | solution.py:276
  25.0 5.7 %collective-permute-start.1 = (bf16[4,1,32,128]{3,2,1,0:T(8,128)(2,1)S(1)}, bf16[4,1,32,128]{3,2,1,0:T(8,128)(2,1)S(1)}, u32[]{:S(2)}, u32[]{:S(2)}) collective-permute-start(bf16[4,1,32,128]{3,2,1,0:T(8,128)(2,1)S(1)} %get-tuple-element.13.head_ref), channel_id=1, source_target_pairs={{64,0},{128,64},{192,128},{256,192},{320,256},{384,320},{448,384},... | collective-permute-start | bytes 98312 | tf_op jit(solution)/shard_map/ppermute | solution.py:277
  27.1 1.0 %copy-start.1 = (bf16[1,4,8,32,128]{4,3,2,1,0:T(8,128)(2,1)S(1)}, bf16[1,4,8,32,128]{4,3,2,1,0:T(8,128)(2,1)}, u32[]{:S(2)}) copy-start(bf16[1,4,8,32,128]{4,3,2,1,0:T(8,128)(2,1)} %param.5) | copy-start | bytes 786436
  29.9 56.7 %copy-start.2 = (bf16[128,128]{1,0:T(8,128)(2,1)S(1)}, bf16[128,128]{1,0:T(8,128)(2,1)}, u32[]{:S(2)}) copy-start(bf16[128,128]{1,0:T(8,128)(2,1)} %constant.9.clone) | copy-start | bytes 98308
  82.6 11.3 %all-to-all-start.4 = ((f32[16,2,128]{2,1,0:T(2,128)}), f32[16,2,128]{2,1,0:T(2,128)S(1)}, u32[]{:S(2)}, u32[]{:S(2)}) async-start(f32[16,2,128]{2,1,0:T(2,128)} %broadcast_in_dim.11), calls=%async_computation.4 | async-start | bytes 32768 | tf_op jit(solution)/shard_map/all_to_all | solution.py:332

commit v5 on v3

--- a/solution.py
+++ b/solution.py
@@ -47,7 +47,7 @@
     return table
 
 
-def reorder_kernel(rows_ref, last_ref, head_ref, out_ref):
+def reorder_kernel(rows_ref, out_ref):
     row = lax.broadcasted_iota(jnp.int32, (128, 128), 0)
     col = lax.broadcasted_iota(jnp.int32, (128, 128), 1)
     table = jnp.where(col == ((row >> 2) & 1) * 64 + (row >> 3) * 4 + (row & 3), 1.0, 0.0).astype(jnp.bfloat16)
@@ -74,11 +74,9 @@
     bias = jnp.broadcast_to(columns_ref[:, TAPS : TAPS + 1], (FILTERS, 128))
     biases_ref[...] = bias
 
-    flat[0:128, :] = jnp.zeros((128, 128), f32)
-    flat[1152:1280, :] = jnp.zeros((128, 128), f32)
     for c in range(CHANNELS):
-        for d in range(1, 9):
-            flat[(d * CHANNELS + c) * 32 : (d * CHANNELS + c + 1) * 32, :] = vol_ref[c, d - 1].astype(f32)
+        for d in range(10):
+            flat[(d * CHANNELS + c) * 32 : (d * CHANNELS + c + 1) * 32, :] = vol_ref[c, d].astype(f32)
     zero_line = jnp.zeros((ROWS, 128), bf16)
     lines[0, :, 0:128] = zero_line
     lines[31, :, 128:256] = zero_line
@@ -265,17 +263,20 @@
     up = [(i, i + 1) for i in range(spaces - 1)]
     down = [(i + 1, i) for i in range(spaces - 1)]
     local = volume[0]
-    last, head = lax.optimization_barrier((local[:, -1:], local[:, :1]))
+    slab = lax.optimization_barrier(jnp.pad(local, ((0, 0), (1, 1), (0, 0), (0, 0))))
+    last, head = slab[:, -2:-1], slab[:, 1:2]
     sent = in_vmem(
         reorder_kernel,
         jax.ShapeDtypeStruct((128, 1024), bf16),
-        (cotangent.reshape(128, 1024), last, head),
+        (cotangent.reshape(128, 1024),),
         megabytes=4,
     )
     cots = lax.all_to_all(sent, "space", split_axis=0, concat_axis=0, tiled=True)
     low = lax.ppermute(last, "space", up)
     high = lax.ppermute(head, "space", down)
-    columns = jnp.concatenate([kernel.astype(f32), bias[:, None]], axis=1)
+    wide = jnp.pad(kernel, ((0, 0), (0, 128 - TAPS))).astype(f32)
+    column = lax.broadcasted_iota(jnp.int32, (FILTERS, 128), 1)
+    columns = jnp.where(column == TAPS, lax.broadcast_in_dim(bias, (FILTERS, 128), (0,)), wide)
     shapes = (
         jax.ShapeDtypeStruct((64, 1024), bf16),
         jax.ShapeDtypeStruct((256, 4096), bf16),
@@ -286,7 +287,7 @@
     inner = in_vmem(
         inner_kernel,
         shapes,
-        (local, columns),
+        (slab, columns),
         (
             pltpu.VMEM((1280, 128), f32),
             pltpu.VMEM((32, ROWS, 256), bf16),
@@ -317,10 +318,13 @@
     out = lax.all_to_all(out, "space", split_axis=0, concat_axis=0, tiled=True)
     pooled = reorder(to_owner, out[:, :1024]).reshape(1, 2, 64, 1024)
     terms = jnp.sum(out[:, 1024:].reshape(spaces, 2, 4, 128).astype(f32), axis=(0, 2))
-    terms = lax.all_to_all(
-        jnp.broadcast_to(terms[None], (batches, 2, 128)), "batch", split_axis=0, concat_axis=0, tiled=True
-    )
-    terms = jnp.sum(terms, axis=0)
+    other = [(i, i ^ 1) for i in range(batches)]
+    cores = [list(range(core, batches, 2)) for core in range(2)]
+    terms = terms + lax.ppermute(terms, "batch", other)
+    copies = jnp.broadcast_to(terms[None], (batches // 2, 2, 128))
+    terms = jnp.sum(
+        lax.all_to_all(copies, "batch", split_axis=0, concat_axis=0, axis_index_groups=cores, tiled=True), axis=0
+    )
     terms = lax.all_to_all(
         jnp.broadcast_to(terms[None], (spaces, 2, 128)), "space", split_axis=0, concat_axis=0, tiled=True
     ).reshape(FILTERS, 128)

time: 92.5 us -> 92.7 us (level)
  blocking collectives: 45.7 us -> 38.8 us
  starting transfers between devices: 27 us -> 33 us
  waiting for transfers between devices: 6.5 us -> 8.23 us
  local copies, waits for them, and re-layouts: 4.07 us -> 2.57 us
    ppermute x0 -> x1, starting transfers between devices: none -> 6 us  [on_device(): terms = terms + lax.ppermute(terms, 'batch', other)]
    all_to_all x1, blocking collectives: 28.5 us -> 22.6 us  [on_device(): lax.all_to_all(copies, 'batch', split_axis=0, concat_axis=0, axis_index_g...]
    pad x0 -> x1, local copies, waits for them, and re-layouts: none -> 0.98 us  [on_device(): jnp.pad(local, ((0, 0), (1, 1), (0, 0), (0, 0)))]
    unnamed x6 -> x4, local copies, waits for them, and re-layouts: 1.91 us -> 0.95 us
    ppermute x1, waiting for transfers between devices: 0.08 us -> 1.02 us  [on_device(): high = lax.ppermute(head, 'space', down)]
    all_to_all x1, blocking collectives: 17.2 us -> 16.2 us  [on_device(): out = lax.all_to_all(out, 'space', split_axis=0, concat_axis=0, tiled=True)]
  transfers between devices with their start and end apart: 4 -> 5, of which waited for: 2 -> 3; matrix products, arithmetic and copies ran while one was open for 3% -> 3% of each run, Pallas kernels for 2% -> 2%
where the time goes in v5:
time: 92.7 us; the launch traced here: 91.3 us
  blocking collectives  38.8 us (42%)
  starting transfers between devices  33 us (36%)
  waiting for transfers between devices  8.23 us (9%)
  Pallas kernels  6.2 us (7%)
  local copies, waits for them, and re-layouts  2.57 us (3%)
    all_to_all x1, blocking collectives, on_device(): lax.all_to_all(copies, 'batch', split_axis=0, concat_axis=0, axis_index_g...  22.6 us
    all_to_all x1, starting transfers between devices, on_device(): lax.all_to_all(sent, 'space', split_axis=0, concat_axis=0, tiled=True)  18.5 us
    all_to_all x1, blocking collectives, on_device(): out = lax.all_to_all(out, 'space', split_axis=0, concat_axis=0, tiled=True)  16.2 us
    all_to_all x1, waiting for transfers between devices, on_device(): lax.all_to_all(jnp.broadcast_to(terms[None], (spaces, 2, 128)), 'space',...  6.41 us
    pallas_call x4, Pallas kernels, in_vmem(): pl.pallas_call(kernel, out_shape=outs, in_specs=[one] * len(operands), ou...  6.2 us
    ppermute x1, starting transfers between devices, on_device(): terms = terms + lax.ppermute(terms, 'batch', other)  6 us
    all_to_all x1, starting transfers between devices, on_device(): lax.all_to_all(jnp.broadcast_to(terms[None], (spaces, 2, 128)), 'space',...  3.95 us
    ppermute x1, starting transfers between devices, on_device(): low = lax.ppermute(last, 'space', up)  3.27 us
  transfers between devices with their start and end apart: 5, of which 3 were waited for; matrix products, arithmetic and copies ran while one was open for 3% of the time, Pallas kernels for 2%

profile of v5, /device:TPU:1, one launch (start us, length us, event | category | flops | bytes accessed | tf_op | source)
XLA Modules:
  0.0 91.3 jit_solution(17387221665329975835)
XLA Ops:
  0.6 0.0 copy-start
  0.6 0.9 %copy-done = bf16[1,2,64,1024]{3,2,1,0:T(8,128)(2,1)S(1)} copy-done((bf16[1,2,64,1024]{3,2,1,0:T(8,128)(2,1)S(1)}, bf16[1,2,64,1024]{3,2,1,0:T(8,128)(2,1)}, u32[]{:S(2)}) %copy-start) | copy-done | bytes 262168
  1.6 0.9 %shard_map.76 = bf16[128,1024]{1,0:T(8,128)(2,1)} custom-call(bf16[128,1024]{1,0:T(8,128)(2,1)S(1)} %bitcast.14), custom_call_target="tpu_custom_call" | custom-call | flops 1000000 | bytes 100000 | tf_op jit(solution)/shard_map/pallas_call | solution.py:242
  2.5 18.5 %all-to-all-start = ((bf16[16,8,1024]{2,1,0:T(8,128)(2,1)}), bf16[16,8,1024]{2,1,0:T(8,128)(2,1)S(1)}, u32[]{:S(2)}, u32[]{:S(2)}) async-start(bf16[16,8,1024]{2,1,0:T(8,128)(2,1)} %bitcast.2), calls=%async_computation | async-start | bytes 524288 | tf_op jit(solution)/shard_map/all_to_all | solution.py:274
  21.0 1.0 %pad.8.vol_ref = bf16[4,10,32,128]{3,2,1,0:T(8,128)(2,1)S(1)} pad(bf16[4,8,32,128]{3,2,1,0:T(8,128)(2,1)} %bitcast.19, bf16[]{:T(256)} %constant.2.clone.1), padding=0_0x1_1x0_0x0_0 | pad | bytes 589826 | tf_op jit(solution)/shard_map/jit(_pad)/pad | solution.py:266
  22.0 3.3 %collective-permute-start = (bf16[4,1,32,128]{3,2,1,0:T(8,128)(2,1)S(1)}, bf16[4,1,32,128]{3,2,1,0:T(8,128)(2,1)S(1)}, u32[]{:S(2)}, u32[]{:S(2)}) collective-permute-start(bf16[4,1,32,128]{3,2,1,0:T(8,128)(2,1)S(1)} %get-tuple-element.18), channel_id=1, source_target_pairs={{0,64},{64,128},{128,192},{192,256},{256,320},{320,384},{384,448},... | collective-permute-start | bytes 98312 | tf_op jit(solution)/shard_map/ppermute | solution.py:275
  25.2 1.3 %collective-permute-start.1 = (bf16[4,1,32,128]{3,2,1,0:T(8,128)(2,1)S(1)}, bf16[4,1,32,128]{3,2,1,0:T(8,128)(2,1)S(1)}, u32[]{:S(2)}, u32[]{:S(2)}) collective-permute-start(bf16[4,1,32,128]{3,2,1,0:T(8,128)(2,1)S(1)} %get-tuple-element.17), channel_id=1, source_target_pairs={{64,0},{128,64},{192,128},{256,192},{320,256},{384,320},{448,384},... | collective-permute-start | bytes 98312 | tf_op jit(solution)/shard_map/ppermute | solution.py:276
  26.5 0.8 convert_select_fusion.columns_ref
  27.3 1.8 %shard_map.77 = (bf16[64,1024]{1,0:T(8,128)(2,1)S(1)}, bf16[256,4096]{1,0:T(8,128)(2,1)S(1)}, bf16[64,1024]{1,0:T(8,128)(2,1)S(1)}, bf16[256,256]{1,0:T(8,128)(2,1)S(1)}, f32[32,128]{1,0:T(8,128)S(1)}) custom-call(bf16[4,10,32,128]{3,2,1,0:T(8,128)(2,1)S(1)} %pad.8.vol_ref, f32[32,128]{1,0:T(8,128)S(1)} %convert_select_fusion.columns_ref), custom_call_target="tpu_custom_call" | custom-call | flops 1000000000 | bytes 5000000 | tf_op jit(solution)/shard_map/pallas_call | solution.py:242
  29.1 0.0 copy-start.1
  29.2 0.0 collective-permute-done.low_ref
  29.2 1.0 %collective-permute-done.1.high_ref = bf16[4,1,32,128]{3,2,1,0:T(8,128)(2,1)S(1)} collective-permute-done((bf16[4,1,32,128]{3,2,1,0:T(8,128)(2,1)S(1)}, bf16[4,1,32,128]{3,2,1,0:T(8,128)(2,1)S(1)}, u32[]{:S(2)}, u32[]{:S(2)}) %collective-permute-start.1) | collective-permute-done | bytes 32800 | tf_op jit(solution)/shard_map/ppermute | solution.py:276
  30.2 0.0 all-to-all-done
  30.2 2.9 %shard_map.78 = bf16[128,1152]{1,0:T(8,128)(2,1)S(1)} custom-call(bf16[4,1,32,128]{3,2,1,0:T(8,128)(2,1)S(1)} %collective-permute-done.low_ref, bf16[4,1,32,128]{3,2,1,0:T(8,128)(2,1)S(1)} %collective-permute-done.1.high_ref, bf16[128,1024]{1,0:T(8,128)(2,1)S(1)} %bitcast.13, bf16[64,1024]{1,0:T(8,128)(2,1)S(1)} %get-tuple-element.10.inner_ref, ...), custom_call_target="tpu_custom_call" | custom-call | flops 600000000 | bytes 5000000 | tf_op jit(solution)/shard_map/pallas_call | solution.py:242
  33.1 16.2 %all_to_all.33 = bf16[16,8,1152]{2,1,0:T(8,128)(2,1)S(1)} all-to-all(bf16[16,8,1152]{2,1,0:T(8,128)(2,1)S(1)} %bitcast.12), channel_id=1, replica_groups=mesh['space'=16,'batch'=64] {'space'}, dimensions={0} | all-to-all | bytes 589824 | tf_op jit(solution)/shard_map/all_to_all | solution.py:318
  49.3 6.0 %collective-permute-start.2 = (f32[2,128]{1,0:T(2,128)S(1)}, f32[2,128]{1,0:T(2,128)S(1)}, u32[]{:S(2)}, u32[]{:S(2)}) collective-permute-start(f32[2,128]{1,0:T(2,128)S(1)} %convert_reduce_fusion), channel_id=1, source_target_pairs={{0,1},{1,0},{2,3},{3,2},{4,5},{5,4},{6,7},{7,6},{8,9},{9,8},{10,11... | collective-permute-start | bytes 3080 | tf_op jit(solution)/shard_map/ppermute | solution.py:323
  55.3 0.8 collective-permute-done.2
  56.1 22.6 %all_to_all.34 = f32[32,2,128]{2,1,0:T(2,128)S(1)} all-to-all(f32[32,2,128]{2,1,0:T(2,128)S(1)} %broadcast_in_dim.7), channel_id=1, replica_groups={{0,2,4,6,8,10,12,14,16,18,20,22,24,26,28,30,32,34,36,38,40,42,44,46,48,..., dimensions={0} | all-to-all | bytes 65536 | tf_op jit(solution)/shard_map/all_to_all | solution.py:326
  78.8 0.6 broadcast_in_dim.8
  79.4 4.0 %all-to-all-start.3 = ((f32[16,2,128]{2,1,0:T(2,128)}), f32[16,2,128]{2,1,0:T(2,128)S(1)}, u32[]{:S(2)}, u32[]{:S(2)}) async-start(f32[16,2,128]{2,1,0:T(2,128)} %broadcast_in_dim.8), calls=%async_computation.3 | async-start | bytes 32768 | tf_op jit(solution)/shard_map/all_to_all | solution.py:328
  83.4 0.0 copy-done.1
  83.4 0.9 %fusion = bf16[128,1024]{1,0:T(8,128)(2,1)} fusion(bf16[128,128]{1,0:T(8,128)(2,1)S(1)} %copy-done.1, bf16[128,1152]{1,0:T(8,128)(2,1)S(1)} %bitcast.17), kind=kOutput, calls=%fused_computation | convolution fusion | flops 33554432 | bytes 557056 | tf_op jit(solution)/shard_map/dot_general | solution.py:254
  84.3 6.4 %all-to-all-done.3 = f32[16,2,128]{2,1,0:T(2,128)S(1)} async-done(((f32[16,2,128]{2,1,0:T(2,128)}), f32[16,2,128]{2,1,0:T(2,128)S(1)}, u32[]{:S(2)}, u32[]{:S(2)}) %all-to-all-start.3) | async-done | bytes 16416 | tf_op jit(solution)/shard_map/all_to_all | solution.py:328
  90.7 0.6 shard_map.79
  (7 shorter events, 0.1 us)
Async XLA Ops:
  0.6 1.0 %copy-start = (bf16[1,2,64,1024]{3,2,1,0:T(8,128)(2,1)S(1)}, bf16[1,2,64,1024]{3,2,1,0:T(8,128)(2,1)}, u32[]{:S(2)}) copy-start(bf16[1,2,64,1024]{3,2,1,0:T(8,128)(2,1)} %param.8) | copy-start | bytes 786436
  2.5 27.7 %all-to-all-start = ((bf16[16,8,1024]{2,1,0:T(8,128)(2,1)}), bf16[16,8,1024]{2,1,0:T(8,128)(2,1)S(1)}, u32[]{:S(2)}, u32[]{:S(2)}) async-start(bf16[16,8,1024]{2,1,0:T(8,128)(2,1)} %bitcast.2), calls=%async_computation | async-start | bytes 524288 | tf_op jit(solution)/shard_map/all_to_all | solution.py:274
  22.0 7.2 %collective-permute-start = (bf16[4,1,32,128]{3,2,1,0:T(8,128)(2,1)S(1)}, bf16[4,1,32,128]{3,2,1,0:T(8,128)(2,1)S(1)}, u32[]{:S(2)}, u32[]{:S(2)}) collective-permute-start(bf16[4,1,32,128]{3,2,1,0:T(8,128)(2,1)S(1)} %get-tuple-element.18), channel_id=1, source_target_pairs={{0,64},{64,128},{128,192},{192,256},{256,320},{320,384},{384,448},... | collective-permute-start | bytes 98312 | tf_op jit(solution)/shard_map/ppermute | solution.py:275
  25.2 5.0 %collective-permute-start.1 = (bf16[4,1,32,128]{3,2,1,0:T(8,128)(2,1)S(1)}, bf16[4,1,32,128]{3,2,1,0:T(8,128)(2,1)S(1)}, u32[]{:S(2)}, u32[]{:S(2)}) collective-permute-start(bf16[4,1,32,128]{3,2,1,0:T(8,128)(2,1)S(1)} %get-tuple-element.17), channel_id=1, source_target_pairs={{64,0},{128,64},{192,128},{256,192},{320,256},{384,320},{448,384},... | collective-permute-start | bytes 98312 | tf_op jit(solution)/shard_map/ppermute | solution.py:276
  29.1 54.2 %copy-start.1 = (bf16[128,128]{1,0:T(8,128)(2,1)S(1)}, bf16[128,128]{1,0:T(8,128)(2,1)}, u32[]{:S(2)}) copy-start(bf16[128,128]{1,0:T(8,128)(2,1)} %constant.9.clone) | copy-start | bytes 98308
  49.3 6.8 %collective-permute-start.2 = (f32[2,128]{1,0:T(2,128)S(1)}, f32[2,128]{1,0:T(2,128)S(1)}, u32[]{:S(2)}, u32[]{:S(2)}) collective-permute-start(f32[2,128]{1,0:T(2,128)S(1)} %convert_reduce_fusion), channel_id=1, source_target_pairs={{0,1},{1,0},{2,3},{3,2},{4,5},{5,4},{6,7},{7,6},{8,9},{9,8},{10,11... | collective-permute-start | bytes 3080 | tf_op jit(solution)/shard_map/ppermute | solution.py:323
  79.4 11.3 %all-to-all-start.3 = ((f32[16,2,128]{2,1,0:T(2,128)}), f32[16,2,128]{2,1,0:T(2,128)S(1)}, u32[]{:S(2)}, u32[]{:S(2)}) async-start(f32[16,2,128]{2,1,0:T(2,128)} %broadcast_in_dim.8), calls=%async_computation.3 | async-start | bytes 32768 | tf_op jit(solution)/shard_map/all_to_all | solution.py:328

commit v6 on v5

--- a/solution.py
+++ b/solution.py
@@ -119,9 +119,36 @@
                 pooled_ref[rows, lane : lane + 128] = (total * 0.125).astype(bf16)
 
 
+def gradients(cots, d2, lane):
+    f32, bf16 = jnp.float32, jnp.bfloat16
+    incoming = cots[d2 * FILTERS : (d2 + 1) * FILTERS, lane : lane + 128].astype(f32) * 0.125
+    return incoming.astype(bf16).astype(f32), (incoming * 0.3).astype(bf16).astype(f32)
+
+
+def middle_kernel(cot_ref, window, code_ref, cots, grads_ref, sums_ref, spread):
+    f32, bf16 = jnp.float32, jnp.bfloat16
+    cots[...] = jnp.dot(depth_table(False), cot_ref[...], preferred_element_type=f32).astype(bf16)
+    bias_sum = jnp.zeros((FILTERS, 128), f32)
+    for plane in range(2):
+        held = slice(plane * FILTERS, (plane + 1) * FILTERS)
+        for tile in range(8):
+            lane = tile * 128
+            first = plane * 1024 + lane
+            full, part = gradients(cots, plane + 1, lane)
+            code = code_ref[held, lane : lane + 128].astype(f32).astype(jnp.int32)
+            for n in range(8):
+                back = jnp.where((code & (1 << n)) != 0, full, part)
+                bias_sum = bias_sum + back
+                spread[n * FILTERS : (n + 1) * FILTERS, first : first + 128] = back.astype(bf16)
+    grads_ref[...] = lax.dot_general(
+        spread[...], window[:, 1024:3072], (((1,), (1,)), ((), ())), preferred_element_type=f32
+    )
+    sums_ref[...] = bias_sum
+
+
 def outer_kernel(
-    low_ref, high_ref, cot_ref, inner_ref, window, code_ref, weights_ref, biases_ref, out_ref,
-    flat, lines, split, edge, spread, pooled, cots
+    low_ref, high_ref, weights_ref, biases_ref, inner_ref, window, cots, grads_ref, sums_ref, out_ref,
+    flat, lines, split, edge, spread, pooled
 ):
     f32, bf16 = jnp.float32, jnp.bfloat16
     for c in range(CHANNELS):
@@ -139,29 +166,8 @@
             lines[j * 8 + h4, :, 128:256] = line
     split[...] = jnp.dot(lines[...].reshape(256, 256).astype(bf16), width_table(), preferred_element_type=f32)
 
-    cots[...] = jnp.dot(depth_table(False), cot_ref[...], preferred_element_type=f32)
-
-    def gradients(d2, lane):
-        incoming = cots[d2 * FILTERS : (d2 + 1) * FILTERS, lane : lane + 128] * 0.125
-        return incoming.astype(bf16).astype(f32), (incoming * 0.3).astype(bf16).astype(f32)
-
-    bias_sum = jnp.zeros((FILTERS, 128), f32)
-    for plane in range(2):
-        rows = slice((plane + 1) * FILTERS, (plane + 2) * FILTERS)
-        held = slice(plane * FILTERS, (plane + 1) * FILTERS)
-        pooled[rows, :] = inner_ref[held, :]
-        for tile in range(8):
-            lane = tile * 128
-            first = (plane + 1) * 1024 + lane
-            full, part = gradients(plane + 1, lane)
-            code = code_ref[held, lane : lane + 128].astype(f32).astype(jnp.int32)
-            for n in range(8):
-                back = jnp.where((code & (1 << n)) != 0, full, part)
-                bias_sum = bias_sum + back
-                spread[n * FILTERS : (n + 1) * FILTERS, first : first + 128] = back.astype(bf16)
-    grads = lax.dot_general(
-        spread[:, 1024:3072], window[:, 1024:3072], (((1,), (1,)), ((), ())), preferred_element_type=f32
-    )
+    pooled[FILTERS : 3 * FILTERS, :] = inner_ref[...]
+    bias_sum, grads = sums_ref[...], grads_ref[...]
 
     sublane = lax.broadcasted_iota(jnp.int32, (8, 128), 0)
     nothing = jnp.zeros((8, 128), f32)
@@ -184,7 +190,7 @@
             conv = jnp.dot(weights_ref[...], edge[:, first : first + 256], preferred_element_type=f32)
             for half in range(2):
                 lane = tile * 256 + half * 128
-                full, part = gradients(d2, lane)
+                full, part = gradients(cots, d2, lane)
                 total = jnp.zeros((FILTERS, 128), f32)
                 for n in range(8):
                     x = conv[n * FILTERS : (n + 1) * FILTERS, half * 128 : (half + 1) * 128] + bias
@@ -192,11 +198,11 @@
                     back = jnp.where(x > 0, full, part)
                     bias_sum = bias_sum + back
                     spread[
-                        n * FILTERS : (n + 1) * FILTERS, d2 * 1024 + lane : d2 * 1024 + lane + 128
+                        n * FILTERS : (n + 1) * FILTERS, side * 1024 + lane : side * 1024 + lane + 128
                     ] = back.astype(bf16)
                 pooled[d2 * FILTERS : (d2 + 1) * FILTERS, lane : lane + 128] = (total * 0.125).astype(bf16)
         grads = grads + lax.dot_general(
-            spread[:, d2 * 1024 : (d2 + 1) * 1024],
+            spread[:, side * 1024 : (side + 1) * 1024],
             edge[:, side * 1024 : (side + 1) * 1024],
             (((1,), (1,)), ((), ())),
             preferred_element_type=f32,
@@ -298,33 +304,42 @@
         flops=1_000_000_000,
         moved=5_000_000,
     )
+    pooled, window, code, weights, biases = inner
+    cots, grads, sums = in_vmem(
+        middle_kernel,
+        (
+            jax.ShapeDtypeStruct((128, 1024), bf16),
+            jax.ShapeDtypeStruct((256, 256), f32),
+            jax.ShapeDtypeStruct((FILTERS, 128), f32),
+        ),
+        (cots, window, code),
+        (pltpu.VMEM((256, 2048), bf16),),
+        flops=300_000_000,
+        moved=3_000_000,
+    )
     out = in_vmem(
         outer_kernel,
         jax.ShapeDtypeStruct((128, 1152), bf16),
-        (low, high, cots, *inner),
+        (low, high, weights, biases, pooled, window, cots, grads, sums),
         (
             pltpu.VMEM((256, 128), f32),
             pltpu.VMEM((32, 8, 256), f32),
             pltpu.VMEM((256, 512), f32),
             pltpu.VMEM((256, 2048), bf16),
-            pltpu.VMEM((256, 4096), bf16),
+            pltpu.VMEM((256, 2048), bf16),
             pltpu.VMEM((128, 1024), bf16),
-            pltpu.VMEM((128, 1024), f32),
         ),
-        flops=600_000_000,
-        moved=5_000_000,
+        flops=400_000_000,
+        moved=4_000_000,
     )
 
     out = lax.all_to_all(out, "space", split_axis=0, concat_axis=0, tiled=True)
     pooled = reorder(to_owner, out[:, :1024]).reshape(1, 2, 64, 1024)
     terms = jnp.sum(out[:, 1024:].reshape(spaces, 2, 4, 128).astype(f32), axis=(0, 2))
-    other = [(i, i ^ 1) for i in range(batches)]
-    cores = [list(range(core, batches, 2)) for core in range(2)]
-    terms = terms + lax.ppermute(terms, "batch", other)
-    copies = jnp.broadcast_to(terms[None], (batches // 2, 2, 128))
-    terms = jnp.sum(
-        lax.all_to_all(copies, "batch", split_axis=0, concat_axis=0, axis_index_groups=cores, tiled=True), axis=0
-    )
+    terms = lax.all_to_all(
+        jnp.broadcast_to(terms[None], (batches, 2, 128)), "batch", split_axis=0, concat_axis=0, tiled=True
+    )
+    terms = jnp.sum(terms, axis=0)
     terms = lax.all_to_all(
         jnp.broadcast_to(terms[None], (spaces, 2, 128)), "space", split_axis=0, concat_axis=0, tiled=True
     ).reshape(FILTERS, 128)

time: 92.7 us -> 89.8 us (0.969)
  starting transfers between devices: 33 us -> 27.7 us
  blocking collectives: 38.8 us -> 43.8 us
  waiting for transfers between devices: 8.23 us -> 6.42 us
    all_to_all x1, blocking collectives: 22.6 us -> 28.6 us  [on_device(): lax.all_to_all(jnp.broadcast_to(terms[None], (batches, 2, 128)), 'batch',...]
    ppermute x1 -> x0, starting transfers between devices: 6 us -> none  [on_device(): terms = terms + lax.ppermute(terms, 'batch', other)]
    ppermute x1, waiting for transfers between devices: 1.02 us -> 0.01 us  [on_device(): high = lax.ppermute(head, 'space', down)]
    all_to_all x1, blocking collectives: 16.2 us -> 15.2 us  [on_device(): out = lax.all_to_all(out, 'space', split_axis=0, concat_axis=0, tiled=True)]
    pallas_call x4 -> x5, Pallas kernels: 6.2 us -> 6.23 us  [in_vmem(): pl.pallas_call(kernel, out_shape=outs, in_specs=[one] * len(operands), ou...]
  transfers between devices with their start and end apart: 5 -> 4, of which waited for: 3 -> 1; matrix products, arithmetic and copies ran while one was open for 3% -> 3% of each run, Pallas kernels for 2% -> 3%
where the time goes in v6:
time: 89.8 us; the launch traced here: 89.3 us
  blocking collectives  43.8 us (49%)
  starting transfers between devices  27.7 us (31%)
  waiting for transfers between devices  6.42 us (7%)
  Pallas kernels  6.23 us (7%)
  local copies, waits for them, and re-layouts  2.58 us (3%)
  matrix products  0.92 us (1%)
    all_to_all x1, blocking collectives, on_device(): lax.all_to_all(jnp.broadcast_to(terms[None], (batches, 2, 128)), 'batch',...  28.6 us
    all_to_all x1, starting transfers between devices, on_device(): lax.all_to_all(sent, 'space', split_axis=0, concat_axis=0, tiled=True)  18.5 us
    all_to_all x1, blocking collectives, on_device(): out = lax.all_to_all(out, 'space', split_axis=0, concat_axis=0, tiled=True)  15.2 us
    all_to_all x1, waiting for transfers between devices, on_device(): lax.all_to_all(jnp.broadcast_to(terms[None], (spaces, 2, 128)), 'space',...  6.41 us
    pallas_call x5, Pallas kernels, in_vmem(): pl.pallas_call(kernel, out_shape=outs, in_specs=[one] * len(operands), ou...  6.23 us
    ppermute x1, starting transfers between devices, on_device(): low = lax.ppermute(last, 'space', up)  3.99 us
    all_to_all x1, starting transfers between devices, on_device(): lax.all_to_all(jnp.broadcast_to(terms[None], (spaces, 2, 128)), 'space',...  3.94 us
  transfers between devices with their start and end apart: 4, of which 1 were waited for; matrix products, arithmetic and copies ran while one was open for 3% of the time, Pallas kernels for 3%

profile of v6, /device:TPU:1, one launch (start us, length us, event | category | flops | bytes accessed | tf_op | source)
XLA Modules:
  0.0 89.3 jit_solution(511023607366860437)
XLA Ops:
  0.6 0.0 copy-start
  0.6 0.9 %copy-done = bf16[1,2,64,1024]{3,2,1,0:T(8,128)(2,1)S(1)} copy-done((bf16[1,2,64,1024]{3,2,1,0:T(8,128)(2,1)S(1)}, bf16[1,2,64,1024]{3,2,1,0:T(8,128)(2,1)}, u32[]{:S(2)}) %copy-start) | copy-done | bytes 262168
  1.6 0.9 %shard_map.77 = bf16[128,1024]{1,0:T(8,128)(2,1)} custom-call(bf16[128,1024]{1,0:T(8,128)(2,1)S(1)} %bitcast.14), custom_call_target="tpu_custom_call" | custom-call | flops 1000000 | bytes 100000 | tf_op jit(solution)/shard_map/pallas_call | solution.py:248
  2.5 18.5 %all-to-all-start = ((bf16[16,8,1024]{2,1,0:T(8,128)(2,1)}), bf16[16,8,1024]{2,1,0:T(8,128)(2,1)S(1)}, u32[]{:S(2)}, u32[]{:S(2)}) async-start(bf16[16,8,1024]{2,1,0:T(8,128)(2,1)} %bitcast.2), calls=%async_computation | async-start | bytes 524288 | tf_op jit(solution)/shard_map/all_to_all | solution.py:280
  21.0 1.0 %pad.8.vol_ref = bf16[4,10,32,128]{3,2,1,0:T(8,128)(2,1)S(1)} pad(bf16[4,8,32,128]{3,2,1,0:T(8,128)(2,1)} %bitcast.19, bf16[]{:T(256)} %constant.2.clone.1), padding=0_0x1_1x0_0x0_0 | pad | bytes 589826 | tf_op jit(solution)/shard_map/jit(_pad)/pad | solution.py:272
  22.0 1.3 %collective-permute-start.1 = (bf16[4,1,32,128]{3,2,1,0:T(8,128)(2,1)S(1)}, bf16[4,1,32,128]{3,2,1,0:T(8,128)(2,1)S(1)}, u32[]{:S(2)}, u32[]{:S(2)}) collective-permute-start(bf16[4,1,32,128]{3,2,1,0:T(8,128)(2,1)S(1)} %get-tuple-element.23), channel_id=1, source_target_pairs={{64,0},{128,64},{192,128},{256,192},{320,256},{384,320},{448,384},... | collective-permute-start | bytes 98312 | tf_op jit(solution)/shard_map/ppermute | solution.py:282
  23.3 4.0 %collective-permute-start = (bf16[4,1,32,128]{3,2,1,0:T(8,128)(2,1)S(1)}, bf16[4,1,32,128]{3,2,1,0:T(8,128)(2,1)S(1)}, u32[]{:S(2)}, u32[]{:S(2)}) collective-permute-start(bf16[4,1,32,128]{3,2,1,0:T(8,128)(2,1)S(1)} %get-tuple-element.24), channel_id=1, source_target_pairs={{0,64},{64,128},{128,192},{192,256},{256,320},{320,384},{384,448},... | collective-permute-start | bytes 98312 | tf_op jit(solution)/shard_map/ppermute | solution.py:281
  27.3 0.8 convert_select_fusion.columns_ref
  28.0 1.8 %shard_map.76 = (bf16[64,1024]{1,0:T(8,128)(2,1)S(1)}, bf16[256,4096]{1,0:T(8,128)(2,1)S(1)}, bf16[64,1024]{1,0:T(8,128)(2,1)S(1)}, bf16[256,256]{1,0:T(8,128)(2,1)S(1)}, f32[32,128]{1,0:T(8,128)S(1)}) custom-call(bf16[4,10,32,128]{3,2,1,0:T(8,128)(2,1)S(1)} %pad.8.vol_ref, f32[32,128]{1,0:T(8,128)S(1)} %convert_select_fusion.columns_ref), custom_call_target="tpu_custom_call" | custom-call | flops 1000000000 | bytes 5000000 | tf_op jit(solution)/shard_map/pallas_call | solution.py:248
  29.9 0.0 all-to-all-done
  29.9 0.9 %shard_map.78 = (bf16[128,1024]{1,0:T(8,128)(2,1)S(1)}, f32[256,256]{1,0:T(8,128)S(1)}, f32[32,128]{1,0:T(8,128)S(1)}) custom-call(bf16[128,1024]{1,0:T(8,128)(2,1)S(1)} %bitcast.13, bf16[256,4096]{1,0:T(8,128)(2,1)S(1)} %get-tuple-element.16.window, bf16[64,1024]{1,0:T(8,128)(2,1)S(1)} %get-tuple-element.17.code_ref), custom_call_target="tpu_custom_call" | custom-call | flops 300000000 | bytes 3000000 | tf_op jit(solution)/shard_map/pallas_call | solution.py:248
  30.8 0.0 collective-permute-done.1.high_ref
  30.8 0.0 collective-permute-done.low_ref
  30.8 0.0 copy-start.1
  30.8 2.0 %shard_map.79 = bf16[128,1152]{1,0:T(8,128)(2,1)S(1)} custom-call(bf16[4,1,32,128]{3,2,1,0:T(8,128)(2,1)S(1)} %collective-permute-done.low_ref, bf16[4,1,32,128]{3,2,1,0:T(8,128)(2,1)S(1)} %collective-permute-done.1.high_ref, bf16[256,256]{1,0:T(8,128)(2,1)S(1)} %get-tuple-element.13.weights_ref, f32[32,128]{1,0:T(8,128)S(1)} %get-tuple-element.14.biases_ref, ...), custom_call_target="tpu_custom_call" | custom-call | flops 400000000 | bytes 4000000 | tf_op jit(solution)/shard_map/pallas_call | solution.py:248
  32.8 15.2 %all_to_all.33 = bf16[16,8,1152]{2,1,0:T(8,128)(2,1)S(1)} all-to-all(bf16[16,8,1152]{2,1,0:T(8,128)(2,1)S(1)} %bitcast.12), channel_id=1, replica_groups=mesh['space'=16,'batch'=64] {'space'}, dimensions={0} | all-to-all | bytes 589824 | tf_op jit(solution)/shard_map/all_to_all | solution.py:336
  48.1 28.6 %all_to_all.34 = f32[64,2,128]{2,1,0:T(2,128)S(1)} all-to-all(f32[64,2,128]{2,1,0:T(2,128)S(1)} %broadcast_in_dim.7), channel_id=1, replica_groups=mesh['space'=16,'batch'=64] {'batch'}, dimensions={0} | all-to-all | bytes 131072 | tf_op jit(solution)/shard_map/all_to_all | solution.py:339
  76.7 0.1 reduce_sum.19
  76.8 0.6 broadcast_in_dim.8
  77.4 3.9 %all-to-all-start.3 = ((f32[16,2,128]{2,1,0:T(2,128)}), f32[16,2,128]{2,1,0:T(2,128)S(1)}, u32[]{:S(2)}, u32[]{:S(2)}) async-start(f32[16,2,128]{2,1,0:T(2,128)} %broadcast_in_dim.8), calls=%async_computation.3 | async-start | bytes 32768 | tf_op jit(solution)/shard_map/all_to_all | solution.py:343
  81.3 0.0 copy-done.1
  81.3 0.9 %fusion = bf16[128,1024]{1,0:T(8,128)(2,1)} fusion(bf16[128,128]{1,0:T(8,128)(2,1)S(1)} %copy-done.1, bf16[128,1152]{1,0:T(8,128)(2,1)S(1)} %bitcast.17), kind=kOutput, calls=%fused_computation | convolution fusion | flops 33554432 | bytes 557056 | tf_op jit(solution)/shard_map/dot_general | solution.py:260
  82.3 6.4 %all-to-all-done.3 = f32[16,2,128]{2,1,0:T(2,128)S(1)} async-done(((f32[16,2,128]{2,1,0:T(2,128)}), f32[16,2,128]{2,1,0:T(2,128)S(1)}, u32[]{:S(2)}, u32[]{:S(2)}) %all-to-all-start.3) | async-done | bytes 16416 | tf_op jit(solution)/shard_map/all_to_all | solution.py:343
  88.7 0.6 shard_map.80
  (5 shorter events, 0.1 us)
Async XLA Ops:
  0.6 1.0 %copy-start = (bf16[1,2,64,1024]{3,2,1,0:T(8,128)(2,1)S(1)}, bf16[1,2,64,1024]{3,2,1,0:T(8,128)(2,1)}, u32[]{:S(2)}) copy-start(bf16[1,2,64,1024]{3,2,1,0:T(8,128)(2,1)} %param.8) | copy-start | bytes 786436
  2.5 27.4 %all-to-all-start = ((bf16[16,8,1024]{2,1,0:T(8,128)(2,1)}), bf16[16,8,1024]{2,1,0:T(8,128)(2,1)S(1)}, u32[]{:S(2)}, u32[]{:S(2)}) async-start(bf16[16,8,1024]{2,1,0:T(8,128)(2,1)} %bitcast.2), calls=%async_computation | async-start | bytes 524288 | tf_op jit(solution)/shard_map/all_to_all | solution.py:280
  22.0 8.8 %collective-permute-start.1 = (bf16[4,1,32,128]{3,2,1,0:T(8,128)(2,1)S(1)}, bf16[4,1,32,128]{3,2,1,0:T(8,128)(2,1)S(1)}, u32[]{:S(2)}, u32[]{:S(2)}) collective-permute-start(bf16[4,1,32,128]{3,2,1,0:T(8,128)(2,1)S(1)} %get-tuple-element.23), channel_id=1, source_target_pairs={{64,0},{128,64},{192,128},{256,192},{320,256},{384,320},{448,384},... | collective-permute-start | bytes 98312 | tf_op jit(solution)/shard_map/ppermute | solution.py:282
  23.3 7.5 %collective-permute-start = (bf16[4,1,32,128]{3,2,1,0:T(8,128)(2,1)S(1)}, bf16[4,1,32,128]{3,2,1,0:T(8,128)(2,1)S(1)}, u32[]{:S(2)}, u32[]{:S(2)}) collective-permute-start(bf16[4,1,32,128]{3,2,1,0:T(8,128)(2,1)S(1)} %get-tuple-element.24), channel_id=1, source_target_pairs={{0,64},{64,128},{128,192},{192,256},{256,320},{320,384},{384,448},... | collective-permute-start | bytes 98312 | tf_op jit(solution)/shard_map/ppermute | solution.py:281
  30.8 50.5 %copy-start.1 = (bf16[128,128]{1,0:T(8,128)(2,1)S(1)}, bf16[128,128]{1,0:T(8,128)(2,1)}, u32[]{:S(2)}) copy-start(bf16[128,128]{1,0:T(8,128)(2,1)} %constant.9.clone) | copy-start | bytes 98308
  77.4 11.3 %all-to-all-start.3 = ((f32[16,2,128]{2,1,0:T(2,128)}), f32[16,2,128]{2,1,0:T(2,128)S(1)}, u32[]{:S(2)}, u32[]{:S(2)}) async-start(f32[16,2,128]{2,1,0:T(2,128)} %broadcast_in_dim.8), calls=%async_computation.3 | async-start | bytes 32768 | tf_op jit(solution)/shard_map/all_to_all | solution.py:343

commit v7 on v6

--- a/solution.py
+++ b/solution.py
@@ -234,6 +234,11 @@
     out_ref[:, 1024:1152] = jnp.dot(depth_table(True), stacked, preferred_element_type=f32).astype(bf16)
 
 
+def share_kernel(parts_ref, copies_ref):
+    total = jnp.sum(parts_ref[...], axis=0)
+    copies_ref[...] = jnp.broadcast_to(total[None], copies_ref.shape)
+
+
 def unpack_kernel(terms_ref, kernel_ref, bias_ref):
     terms = terms_ref[...]
     kernel_ref[...] = terms[:, :TAPS]
@@ -339,10 +344,8 @@
     terms = lax.all_to_all(
         jnp.broadcast_to(terms[None], (batches, 2, 128)), "batch", split_axis=0, concat_axis=0, tiled=True
     )
-    terms = jnp.sum(terms, axis=0)
-    terms = lax.all_to_all(
-        jnp.broadcast_to(terms[None], (spaces, 2, 128)), "space", split_axis=0, concat_axis=0, tiled=True
-    ).reshape(FILTERS, 128)
+    copies = in_vmem(share_kernel, jax.ShapeDtypeStruct((spaces, 2, 128), f32), (terms,), megabytes=4)
+    terms = lax.all_to_all(copies, "space", split_axis=0, concat_axis=0, tiled=True).reshape(FILTERS, 128)
     kernel_grad, bias_grad = in_vmem(
         unpack_kernel,
         (jax.ShapeDtypeStruct((FILTERS, TAPS), f32), jax.ShapeDtypeStruct((1, FILTERS), f32)),

time: 89.8 us -> 89.7 us (level)
    pallas_call x5 -> x6, Pallas kernels: 6.23 us -> 6.91 us  [in_vmem(): pl.pallas_call(kernel, out_shape=outs, in_specs=[one] * len(operands), ou...]
where the time goes in v7:
time: 89.7 us; the launch traced here: 89.3 us
  blocking collectives  43.8 us (49%)
  starting transfers between devices  27.7 us (31%)
  Pallas kernels  6.91 us (8%)
  waiting for transfers between devices  6.42 us (7%)
  local copies, waits for them, and re-layouts  1.96 us (2%)
  matrix products  0.92 us (1%)
    all_to_all x1, blocking collectives, on_device(): lax.all_to_all(jnp.broadcast_to(terms[None], (batches, 2, 128)), 'batch',...  28.6 us
    all_to_all x1, starting transfers between devices, on_device(): lax.all_to_all(sent, 'space', split_axis=0, concat_axis=0, tiled=True)  18.5 us
    all_to_all x1, blocking collectives, on_device(): out = lax.all_to_all(out, 'space', split_axis=0, concat_axis=0, tiled=True)  15.2 us
    pallas_call x6, Pallas kernels, in_vmem(): pl.pallas_call(kernel, out_shape=outs, in_specs=[one] * len(operands), ou...  6.91 us
    all_to_all x1, waiting for transfers between devices, on_device(): lax.all_to_all(copies, 'space', split_axis=0, concat_axis=0, tiled=True)  6.41 us
    ppermute x1, starting transfers between devices, on_device(): low = lax.ppermute(last, 'space', up)  3.99 us
    all_to_all x1, starting transfers between devices, on_device(): lax.all_to_all(copies, 'space', split_axis=0, concat_axis=0, tiled=True)  3.94 us
  transfers between devices with their start and end apart: 4, of which 1 were waited for; matrix products, arithmetic and copies ran while one was open for 3% of the time, Pallas kernels for 3%

profile of v7, /device:TPU:1, one launch (start us, length us, event | category | flops | bytes accessed | tf_op | source)
XLA Modules:
  0.0 89.3 jit_solution(11455216142329741579)
XLA Ops:
  0.6 0.0 copy-start
  0.6 0.9 %copy-done = bf16[1,2,64,1024]{3,2,1,0:T(8,128)(2,1)S(1)} copy-done((bf16[1,2,64,1024]{3,2,1,0:T(8,128)(2,1)S(1)}, bf16[1,2,64,1024]{3,2,1,0:T(8,128)(2,1)}, u32[]{:S(2)}) %copy-start) | copy-done | bytes 262168
  1.6 0.9 %shard_map.77 = bf16[128,1024]{1,0:T(8,128)(2,1)} custom-call(bf16[128,1024]{1,0:T(8,128)(2,1)S(1)} %bitcast.14), custom_call_target="tpu_custom_call" | custom-call | flops 1000000 | bytes 100000 | tf_op jit(solution)/shard_map/pallas_call | solution.py:253
  2.5 18.5 %all-to-all-start = ((bf16[16,8,1024]{2,1,0:T(8,128)(2,1)}), bf16[16,8,1024]{2,1,0:T(8,128)(2,1)S(1)}, u32[]{:S(2)}, u32[]{:S(2)}) async-start(bf16[16,8,1024]{2,1,0:T(8,128)(2,1)} %bitcast.2), calls=%async_computation | async-start | bytes 524288 | tf_op jit(solution)/shard_map/all_to_all | solution.py:285
  21.0 1.0 %pad.8.vol_ref = bf16[4,10,32,128]{3,2,1,0:T(8,128)(2,1)S(1)} pad(bf16[4,8,32,128]{3,2,1,0:T(8,128)(2,1)} %bitcast.19, bf16[]{:T(256)} %constant.2.clone.1), padding=0_0x1_1x0_0x0_0 | pad | bytes 589826 | tf_op jit(solution)/shard_map/jit(_pad)/pad | solution.py:277
  22.0 1.3 %collective-permute-start.1 = (bf16[4,1,32,128]{3,2,1,0:T(8,128)(2,1)S(1)}, bf16[4,1,32,128]{3,2,1,0:T(8,128)(2,1)S(1)}, u32[]{:S(2)}, u32[]{:S(2)}) collective-permute-start(bf16[4,1,32,128]{3,2,1,0:T(8,128)(2,1)S(1)} %get-tuple-element.23), channel_id=1, source_target_pairs={{64,0},{128,64},{192,128},{256,192},{320,256},{384,320},{448,384},... | collective-permute-start | bytes 98312 | tf_op jit(solution)/shard_map/ppermute | solution.py:287
  23.3 4.0 %collective-permute-start = (bf16[4,1,32,128]{3,2,1,0:T(8,128)(2,1)S(1)}, bf16[4,1,32,128]{3,2,1,0:T(8,128)(2,1)S(1)}, u32[]{:S(2)}, u32[]{:S(2)}) collective-permute-start(bf16[4,1,32,128]{3,2,1,0:T(8,128)(2,1)S(1)} %get-tuple-element.24), channel_id=1, source_target_pairs={{0,64},{64,128},{128,192},{192,256},{256,320},{320,384},{384,448},... | collective-permute-start | bytes 98312 | tf_op jit(solution)/shard_map/ppermute | solution.py:286
  27.3 0.8 convert_select_fusion.columns_ref
  28.0 1.8 %shard_map.76 = (bf16[64,1024]{1,0:T(8,128)(2,1)S(1)}, bf16[256,4096]{1,0:T(8,128)(2,1)S(1)}, bf16[64,1024]{1,0:T(8,128)(2,1)S(1)}, bf16[256,256]{1,0:T(8,128)(2,1)S(1)}, f32[32,128]{1,0:T(8,128)S(1)}) custom-call(bf16[4,10,32,128]{3,2,1,0:T(8,128)(2,1)S(1)} %pad.8.vol_ref, f32[32,128]{1,0:T(8,128)S(1)} %convert_select_fusion.columns_ref), custom_call_target="tpu_custom_call" | custom-call | flops 1000000000 | bytes 5000000 | tf_op jit(solution)/shard_map/pallas_call | solution.py:253
  29.9 0.0 all-to-all-done
  29.9 0.9 %shard_map.78 = (bf16[128,1024]{1,0:T(8,128)(2,1)S(1)}, f32[256,256]{1,0:T(8,128)S(1)}, f32[32,128]{1,0:T(8,128)S(1)}) custom-call(bf16[128,1024]{1,0:T(8,128)(2,1)S(1)} %bitcast.13, bf16[256,4096]{1,0:T(8,128)(2,1)S(1)} %get-tuple-element.16.window, bf16[64,1024]{1,0:T(8,128)(2,1)S(1)} %get-tuple-element.17.code_ref), custom_call_target="tpu_custom_call" | custom-call | flops 300000000 | bytes 3000000 | tf_op jit(solution)/shard_map/pallas_call | solution.py:253
  30.8 0.0 collective-permute-done.1.high_ref
  30.8 0.0 collective-permute-done.low_ref
  30.8 0.0 copy-start.1
  30.8 2.0 %shard_map.79 = bf16[128,1152]{1,0:T(8,128)(2,1)S(1)} custom-call(bf16[4,1,32,128]{3,2,1,0:T(8,128)(2,1)S(1)} %collective-permute-done.low_ref, bf16[4,1,32,128]{3,2,1,0:T(8,128)(2,1)S(1)} %collective-permute-done.1.high_ref, bf16[256,256]{1,0:T(8,128)(2,1)S(1)} %get-tuple-element.13.weights_ref, f32[32,128]{1,0:T(8,128)S(1)} %get-tuple-element.14.biases_ref, ...), custom_call_target="tpu_custom_call" | custom-call | flops 400000000 | bytes 4000000 | tf_op jit(solution)/shard_map/pallas_call | solution.py:253
  32.8 15.2 %all_to_all.33 = bf16[16,8,1152]{2,1,0:T(8,128)(2,1)S(1)} all-to-all(bf16[16,8,1152]{2,1,0:T(8,128)(2,1)S(1)} %bitcast.12), channel_id=1, replica_groups=mesh['space'=16,'batch'=64] {'space'}, dimensions={0} | all-to-all | bytes 589824 | tf_op jit(solution)/shard_map/all_to_all | solution.py:341
  48.1 28.6 %all_to_all.34.parts_ref = f32[64,2,128]{2,1,0:T(2,128)S(1)} all-to-all(f32[64,2,128]{2,1,0:T(2,128)S(1)} %broadcast_in_dim.10), channel_id=1, replica_groups=mesh['space'=16,'batch'=64] {'batch'}, dimensions={0} | all-to-all | bytes 131072 | tf_op jit(solution)/shard_map/all_to_all | solution.py:344
  76.7 0.7 shard_map.80
  77.4 3.9 %all-to-all-start.3 = ((f32[16,2,128]{2,1,0:T(2,128)}), f32[16,2,128]{2,1,0:T(2,128)S(1)}, u32[]{:S(2)}, u32[]{:S(2)}) async-start(f32[16,2,128]{2,1,0:T(2,128)} %shard_map.80), calls=%async_computation.3 | async-start | bytes 32768 | tf_op jit(solution)/shard_map/all_to_all | solution.py:348
  81.3 0.0 copy-done.1
  81.3 0.9 %fusion = bf16[128,1024]{1,0:T(8,128)(2,1)} fusion(bf16[128,128]{1,0:T(8,128)(2,1)S(1)} %copy-done.1, bf16[128,1152]{1,0:T(8,128)(2,1)S(1)} %bitcast.17), kind=kOutput, calls=%fused_computation | convolution fusion | flops 33554432 | bytes 557056 | tf_op jit(solution)/shard_map/dot_general | solution.py:265
  82.2 6.4 %all-to-all-done.3 = f32[16,2,128]{2,1,0:T(2,128)S(1)} async-done(((f32[16,2,128]{2,1,0:T(2,128)}), f32[16,2,128]{2,1,0:T(2,128)S(1)}, u32[]{:S(2)}, u32[]{:S(2)}) %all-to-all-start.3) | async-done | bytes 16416 | tf_op jit(solution)/shard_map/all_to_all | solution.py:348
  88.7 0.6 shard_map.81
  (5 shorter events, 0.1 us)
Async XLA Ops:
  0.6 1.0 %copy-start = (bf16[1,2,64,1024]{3,2,1,0:T(8,128)(2,1)S(1)}, bf16[1,2,64,1024]{3,2,1,0:T(8,128)(2,1)}, u32[]{:S(2)}) copy-start(bf16[1,2,64,1024]{3,2,1,0:T(8,128)(2,1)} %param.8) | copy-start | bytes 786436
  2.5 27.4 %all-to-all-start = ((bf16[16,8,1024]{2,1,0:T(8,128)(2,1)}), bf16[16,8,1024]{2,1,0:T(8,128)(2,1)S(1)}, u32[]{:S(2)}, u32[]{:S(2)}) async-start(bf16[16,8,1024]{2,1,0:T(8,128)(2,1)} %bitcast.2), calls=%async_computation | async-start | bytes 524288 | tf_op jit(solution)/shard_map/all_to_all | solution.py:285
  22.0 8.8 %collective-permute-start.1 = (bf16[4,1,32,128]{3,2,1,0:T(8,128)(2,1)S(1)}, bf16[4,1,32,128]{3,2,1,0:T(8,128)(2,1)S(1)}, u32[]{:S(2)}, u32[]{:S(2)}) collective-permute-start(bf16[4,1,32,128]{3,2,1,0:T(8,128)(2,1)S(1)} %get-tuple-element.23), channel_id=1, source_target_pairs={{64,0},{128,64},{192,128},{256,192},{320,256},{384,320},{448,384},... | collective-permute-start | bytes 98312 | tf_op jit(solution)/shard_map/ppermute | solution.py:287
  23.3 7.5 %collective-permute-start = (bf16[4,1,32,128]{3,2,1,0:T(8,128)(2,1)S(1)}, bf16[4,1,32,128]{3,2,1,0:T(8,128)(2,1)S(1)}, u32[]{:S(2)}, u32[]{:S(2)}) collective-permute-start(bf16[4,1,32,128]{3,2,1,0:T(8,128)(2,1)S(1)} %get-tuple-element.24), channel_id=1, source_target_pairs={{0,64},{64,128},{128,192},{192,256},{256,320},{320,384},{384,448},... | collective-permute-start | bytes 98312 | tf_op jit(solution)/shard_map/ppermute | solution.py:286
  30.8 50.5 %copy-start.1 = (bf16[128,128]{1,0:T(8,128)(2,1)S(1)}, bf16[128,128]{1,0:T(8,128)(2,1)}, u32[]{:S(2)}) copy-start(bf16[128,128]{1,0:T(8,128)(2,1)} %constant.9.clone) | copy-start | bytes 98308
  77.4 11.3 %all-to-all-start.3 = ((f32[16,2,128]{2,1,0:T(2,128)}), f32[16,2,128]{2,1,0:T(2,128)S(1)}, u32[]{:S(2)}, u32[]{:S(2)}) async-start(f32[16,2,128]{2,1,0:T(2,128)} %shard_map.80), calls=%async_computation.3 | async-start | bytes 32768 | tf_op jit(solution)/shard_map/all_to_all | solution.py:348
